TPU v7x, 128 devices: a whole 4x4x4 slice. The times are simulated.
128 devices in a mesh: gx: 16 (over z, y), gy: 8 (over x, core).
Axes of the slice: x: 4, y: 4, z: 4, core: 2. Of those that a mesh axis runs over, the one named last changes fastest.
Arguments:
- atmospheric_constituents: float32 [5, 72, 64, 2048], P(None, None, 'gy', 'gx'), may hold values from 0.001 to 2
- thermal_ratio: float32 [72, 64, 2048], P(None, 'gy', 'gx'), may hold values from 0.5 to 1.5
- flow_velocity: float32 [2, 72, 64, 2048], P(None, None, 'gy', 'gx'), may hold values from -4 to 4
- solar_elevation_factor: float32 [64, 2048], P('gy', 'gx'), may hold values from 0.1 to 1
- ground_reflectivity: float32 [64, 2048], P('gy', 'gx'), may hold values from 0.05 to 0.6
- sunlit_indicator: int32 [64, 2048], P('gy', 'gx'), may hold values from 0 to 1, as said below
- molecular_optics_lookup: float32 [3, 112, 72], replicated, may hold values from 0.0001 to 0.05
- condensate_optics_lookup: float32 [7, 112], replicated, may hold values from 0.1 to 0.9
Outputs:
- radiative_warming_rate: float32 [72, 64, 2048], P(None, 'gy', 'gx')
- advected_thermal_ratio: float32 [72, 64, 2048], P(None, 'gy', 'gx')
Inputs may be any that keep to these rules, and one draw needn't show every extreme that they name: `sunlit_indicator`: A column's flag and that of the column 1024 further along the last dimension in the same row (round the end) sum to one.
All inputs are finite; a program needn't handle non-finite values.
Results may differ from a plain program's by a relative error of at most 0.0003.
Values sent between devices are 32-bit elements; how exact they have to be, the bound alone decides.
A program may use at most 128 MiB of HBM per device.

v0:
```python
import jax
import jax.numpy as jnp
import numpy as np
from jax import lax
from jax.sharding import PartitionSpec as P

NODES = 4


TIME_INCREMENT = 0.05


def shifted(value, axis, steps):
    count = lax.axis_size(axis)
    pairs = [(source, (source + steps) % count) for source in range(count)]
    return lax.ppermute(value, axis, pairs)


def padded_2(block, sides, width):
    for axis, dim in sides:
        count = lax.axis_size(axis)
        forward = [(i, i + 1) for i in range(count - 1)]
        forward.append((count - 1, 0))
        backward = [(target, source) for source, target in forward]
        low = lax.ppermute(
            lax.slice_in_dim(block, block.shape[dim] - width, None, axis=dim), axis, forward
        )
        high = lax.ppermute(lax.slice_in_dim(block, 0, width, axis=dim), axis, backward)
        block = jnp.concatenate([low, block, high], axis=dim)
    return block


def gll_derivative():
    points = np.array([-1.0, -1.0 / np.sqrt(5.0), 1.0 / np.sqrt(5.0), 1.0])
    legendre = 0.5 * (5.0 * points**3 - 3.0 * points)
    derivative = np.zeros((4, 4))
    for source in range(4):
        for target in range(4):
            if source != target:
                derivative[source, target] = legendre[source] / (
                    legendre[target] * (points[source] - points[target])
                )
    derivative[0, 0] = -3.0
    derivative[3, 3] = 3.0
    return derivative


def depth_terms(coeffs, optics_table, columns):
    vapour, ozone_amount, thickness, liquid, frozen, temper = columns
    weighted = thickness * temper * temper
    gas_depth = (
        coeffs[0][:, None] * (weighted * vapour)[None, :]
        + coeffs[1][:, None] * (weighted * ozone_amount)[None, :]
    )
    rayleigh = coeffs[2][:, None] * thickness[None, :]
    liquid_depth = optics_table[0][:, None] * liquid[None, :]
    ice_depth = optics_table[3][:, None] * frozen[None, :]
    liquid_scatter = optics_table[1][:, None] * liquid_depth
    ice_scatter = optics_table[4][:, None] * ice_depth
    scattering = rayleigh + liquid_scatter + ice_scatter
    absorption = gas_depth + (liquid_depth - liquid_scatter) + (ice_depth - ice_scatter)
    forward = optics_table[2][:, None] * liquid_scatter + optics_table[5][:, None] * ice_scatter
    return (scattering, absorption, forward)


def layer_optics(coeffs, optics_table, columns, cosine):
    scattering, absorption, forward = depth_terms(coeffs, optics_table, columns)
    optical_depth = scattering + absorption
    single_albedo = scattering / optical_depth
    asymmetry = forward / scattering
    eigen_rate = 2.0 * jnp.sqrt(absorption / optical_depth * (1.0 - single_albedo * asymmetry))
    gamma_one = 2.0 - single_albedo * (1.0 + asymmetry)
    gamma_two = single_albedo * (1.0 - asymmetry)
    shrink = jnp.expm1(-eigen_rate * optical_depth)
    decay_factor = 1.0 + shrink
    spread = -shrink * (2.0 + shrink)
    denominator = gamma_one * spread + eigen_rate * (1.0 + decay_factor * decay_factor)
    reflect = gamma_two * spread / denominator
    transmit = 2.0 * eigen_rate * decay_factor / denominator
    beam_loss = jnp.expm1(-optical_depth / cosine[None, :])
    reflect_beam = -0.5 * single_albedo * beam_loss * (1.0 - asymmetry)
    transmit_beam = -0.5 * single_albedo * beam_loss * (1.0 + asymmetry)
    return (reflect, transmit, reflect_beam, transmit_beam)


def block_nets(coeffs, optics_table, columns, cosine, ground):
    solar_weight = optics_table[6][:, None]
    plane = (optics_table.shape[1], cosine.shape[0])

    def beam_step(beam_flux, per_level):
        scattering, absorption, unused = depth_terms(per_level[0], optics_table, per_level[1:])
        direct = 1.0 + jnp.expm1(-(scattering + absorption) / cosine[None, :])
        return (beam_flux * direct, beam_flux)

    surface_beam, beams = lax.scan(
        beam_step, jnp.broadcast_to(cosine[None, :], plane), (coeffs,) + columns, unroll=8
    )
    ground_full = jnp.broadcast_to(ground[None, :], plane)

    def below_step(below, per_level):
        albedo_below, source_below = below
        beam_now = per_level[-1]
        reflect, transmit, reflect_beam, transmit_beam = layer_optics(
            per_level[0], optics_table, per_level[1:-1], cosine
        )
        inverse = 1.0 / (1.0 - reflect * albedo_below)
        albedo_here = reflect + transmit * transmit * albedo_below * inverse
        source_here = beam_now * reflect_beam + transmit * inverse * (
            source_below + albedo_below * beam_now * transmit_beam
        )
        gain_coef = transmit * inverse
        offset = inverse * (beam_now * transmit_beam + reflect * source_below)
        weight = solar_weight * (1.0 - albedo_below)
        upper_part = jnp.sum(solar_weight * (beam_now - source_here), axis=0)
        return ((albedo_here, source_here), (gain_coef, offset, weight, upper_part))

    unused_carry, (gains, offsets, weights, uppers) = lax.scan(
        below_step,
        (ground_full, ground_full * surface_beam),
        (coeffs,) + columns + (beams,),
        reverse=True,
        unroll=8,
    )

    def down_step(diffuse_now, per_level):
        gain_coef, offset, weight = per_level
        diffuse_new = gain_coef * diffuse_now + offset
        return (diffuse_new, jnp.sum(weight * diffuse_new, axis=0))

    unused_last, lowers = lax.scan(
        down_step, jnp.zeros(plane, jnp.float32), (gains, offsets, weights), unroll=8
    )
    bottom = jnp.sum(solar_weight * (surface_beam - ground_full * surface_beam), axis=0)
    upper_all = jnp.concatenate([uppers, bottom[None]], axis=0)
    lower_all = jnp.concatenate([jnp.zeros_like(bottom)[None], lowers], axis=0)
    return upper_all + lower_all


def shortwave(
    state_cols, temp_cols, cosine, ground, molecular_optics_lookup, condensate_optics_lookup
):
    gpoints = molecular_optics_lookup.shape[1]
    level_sum_entries = molecular_optics_lookup.shape[2]
    blocks = gpoints // 56
    group_width = gpoints // blocks
    gas_blocks = molecular_optics_lookup.reshape(
        3, blocks, group_width, level_sum_entries
    ).transpose(1, 3, 0, 2)
    table_blocks = condensate_optics_lookup.reshape(7, blocks, group_width).transpose(1, 0, 2)
    columns = (state_cols[0], state_cols[1], state_cols[2], state_cols[3], state_cols[4], temp_cols)

    def one_block(running, per_block):
        return (running + block_nets(per_block[0], per_block[1], columns, cosine, ground), 0.0)

    nets, unused = lax.scan(
        one_block,
        jnp.zeros((level_sum_entries + 1, cosine.shape[0]), jnp.float32),
        (gas_blocks, table_blocks),
    )
    return level_sum_entries / gpoints * (nets[:-1] - nets[1:])


def pair_average(values, before, beyond, node_index):
    return jnp.where(
        node_index == NODES - 1,
        0.5 * (values + beyond),
        jnp.where(node_index == 0, 0.5 * (before + values), values),
    )


def local(
    atmospheric_constituents,
    thermal_ratio,
    flow_velocity,
    solar_elevation_factor,
    ground_reflectivity,
    sunlit_indicator,
    molecular_optics_lookup,
    condensate_optics_lookup,
):
    level_sum_entries, resident_line_number, resident_span_size = thermal_ratio.shape
    resident_profile_number = resident_line_number * resident_span_size
    half_cols = resident_profile_number // 2
    flat_state = atmospheric_constituents.reshape(5, level_sum_entries, resident_profile_number)
    thermal_ratio_vector = thermal_ratio.reshape(level_sum_entries, resident_profile_number)
    cosine = solar_elevation_factor.reshape(resident_profile_number)
    ground = ground_reflectivity.reshape(resident_profile_number)
    day_flags = sunlit_indicator.reshape(resident_profile_number)
    surface_here = jnp.stack([cosine, ground])
    day_count = jnp.sum(day_flags)
    sent_count = day_count // 2
    kept_count = day_count - sent_count
    incoming = (resident_profile_number - day_count) // 2
    rank_end = jnp.cumsum(day_flags)
    slot_ids = jnp.arange(resident_profile_number, dtype=jnp.int32)
    located = jnp.minimum(
        jnp.searchsorted(rank_end, slot_ids, side="right"), resident_profile_number - 1
    )
    half_ids = slot_ids[:half_cols]
    outgoing_source_start = located[:half_cols]
    outgoing_sunlit_flags = half_ids < sent_count
    send_state = jnp.where(
        outgoing_sunlit_flags, jnp.take(flat_state, outgoing_source_start, axis=2), 0.0
    )
    outgoing_thermal_ratio = jnp.where(
        outgoing_sunlit_flags, jnp.take(thermal_ratio_vector, outgoing_source_start, axis=1), 0.0
    )
    send_surface = jnp.where(
        outgoing_sunlit_flags, jnp.take(surface_here, outgoing_source_start, axis=1), 0.0
    )
    partner = lax.axis_size("gx") // 2
    got_state, got_temp, got_surface = shifted(
        (send_state, outgoing_thermal_ratio, send_surface), "gx", partner
    )
    from_own = half_ids < kept_count
    retained_source_start = jnp.take(
        located, jnp.minimum(sent_count + half_ids, resident_profile_number - 1)
    )
    recv_from = jnp.clip(half_ids - kept_count, 0, half_cols - 1)
    work_state = jnp.where(
        from_own,
        jnp.take(flat_state, retained_source_start, axis=2),
        jnp.take(got_state, recv_from, axis=2),
    )
    work_temp = jnp.where(
        from_own,
        jnp.take(thermal_ratio_vector, retained_source_start, axis=1),
        jnp.take(got_temp, recv_from, axis=1),
    )
    work_surface = jnp.where(
        from_own,
        jnp.take(surface_here, retained_source_start, axis=1),
        jnp.take(got_surface, recv_from, axis=1),
    )
    work_heat = shortwave(
        work_state,
        work_temp,
        work_surface[0],
        work_surface[1],
        molecular_optics_lookup,
        condensate_optics_lookup,
    )
    back_from = jnp.minimum(kept_count + half_ids, half_cols - 1)
    send_back = jnp.where(half_ids < incoming, jnp.take(work_heat, back_from, axis=1), 0.0)
    returned = shifted(send_back, "gx", partner)
    rank_here = rank_end - 1
    went_away = rank_here < sent_count
    heat_flat = jnp.where(
        went_away,
        jnp.take(returned, jnp.clip(rank_here, 0, half_cols - 1), axis=1),
        jnp.take(work_heat, jnp.clip(rank_here - sent_count, 0, half_cols - 1), axis=1),
    )
    heat_flat = jnp.where(day_flags == 1, heat_flat, 0.0)
    radiative_warming_rate = heat_flat.reshape(
        level_sum_entries, resident_line_number, resident_span_size
    )
    derivative = gll_derivative()
    x_derivative = jnp.asarray(
        np.kron(np.eye(resident_span_size // NODES), derivative).T, jnp.float32
    )
    y_derivative = jnp.asarray(
        np.kron(np.eye(resident_line_number // NODES), derivative), jnp.float32
    )
    x_nodes = (jnp.arange(resident_span_size) % NODES)[None, None, :]
    y_nodes = (jnp.arange(resident_line_number) % NODES)[None, :, None]

    def averaged(values):
        padded = padded_2(values, (("gx", 2),), 1)
        along_x = pair_average(values, padded[:, :, :-2], padded[:, :, 2:], x_nodes)
        padded_y = padded_2(along_x, (("gy", 1),), 1)
        return pair_average(along_x, padded_y[:, :-2], padded_y[:, 2:], y_nodes)

    def warming_change_rate(field_now):
        slope_x = jnp.dot(
            field_now.reshape(-1, resident_span_size), x_derivative, precision=lax.Precision.HIGHEST
        ).reshape(field_now.shape)
        slope_y = jnp.einsum(
            "ij,ljx->lix", y_derivative, field_now, precision=lax.Precision.HIGHEST
        )
        return averaged(
            radiative_warming_rate - (flow_velocity[0] * slope_x + flow_velocity[1] * slope_y)
        )

    opening_advection_part = thermal_ratio + TIME_INCREMENT * warming_change_rate(thermal_ratio)
    middle_advection_part = 0.75 * thermal_ratio + 0.25 * (
        opening_advection_part + TIME_INCREMENT * warming_change_rate(opening_advection_part)
    )
    advected_thermal_ratio = 1.0 / 3.0 * thermal_ratio + 2.0 / 3.0 * (
        middle_advection_part + TIME_INCREMENT * warming_change_rate(middle_advection_part)
    )
    return (radiative_warming_rate, advected_thermal_ratio)


def solution(mesh):
    in_specs = (
        P(None, None, "gy", "gx"),
        P(None, "gy", "gx"),
        P(None, None, "gy", "gx"),
        P("gy", "gx"),
        P("gy", "gx"),
        P("gy", "gx"),
        P(),
        P(),
    )
    out_specs = (P(None, "gy", "gx"), P(None, "gy", "gx"))
    return jax.shard_map(local, mesh=mesh, in_specs=in_specs, out_specs=out_specs, check_vma=False)
```

profile of v0, /device:TPU:1, one launch (start us, length us, event | category | flops | bytes accessed | tf_op | source)
XLA Modules:
  0.0 746.8 jit_solution(15528764937539521717)
XLA Ops:
  7.6 50.7 %while.169 = (s32[]{:T(128)}, u32[1024]{0:T(1024)S(1)}, u32[1024]{0:T(1024)S(1)}, s32[1024]{0:T(1024)S(1)}, s32[]{:T(128)}, /*index=5*/s32[]{:T(128)}, s32[]{}) while((s32[]{:T(128)}, u32[1024]{0:T(1024)S(1)}, u32[1024]{0:T(1024)S(1)}, s32[1024]{0:T(1024)S(1)}, s32[]{:T(128)}, /*index=5*/s32[]{:T(128)}, s32[]{}) %tuple.522), condition=%wide.region_4.5_spmd.clone, body=%wide.region_3.4_spmd.clone.sunk | while | flops 19460 | bytes 63589 | solution.py:197
  7.6 4.5 gather_fusion
  12.3 4.5 gather_fusion
  16.9 4.5 gather_fusion
  21.5 4.5 gather_fusion
  26.1 4.5 gather_fusion
  30.7 4.5 gather_fusion
  35.3 4.5 gather_fusion
  39.9 4.5 gather_fusion
  44.5 4.5 gather_fusion
  49.1 4.5 gather_fusion
  53.8 4.5 gather_fusion
  58.4 3.2 copy.77
  61.6 4.6 gather_fusion.7
  66.8 3.8 bitcast_select_fusion.1
  72.0 4.4 collective-permute-start.1
  81.5 3.0 collective-permute-start
  90.6 4.5 gather_fusion.6
  99.0 5.2 collective-permute-done
  110.3 3.9 gather_fusion.3
  114.2 6.0 bitcast_select_fusion
  121.9 553.0 %while.173 = (s32[]{:T(128)}, f32[73,512]{1,0:T(8,128)S(1)}, f32[1,512]{1,0:T(1,128)S(1)}, f32[1,512]{1,0:T(1,128)S(1)}, f32[2,72,3,56]{1,3,0,2:T(8,128)S(1)}, /...) while((s32[]{:T(128)}, f32[73,512]{1,0:T(8,128)S(1)}, ...), condition=%wide.region_29.34_spmd.clone, body=%wide.region_5.33_spmd.clone.sunk | while | flops 48399896 | bytes 59970308 | solution.py:155
  122.2 4.2 broadcast.994.clone
  126.5 30.6 %while.174 = (s32[]{:T(128)}, f32[56,512]{1,0:T(8,128)S(1)}, f32[9,8,56,512]{3,2,1,0:T(8,128)}, f32[9,8,3,56]{3,2,1,0:T(4,128)S(1)}, f32[9,8,512]{2,1,0:T(8,128)...) while((s32[]{:T(128)}, f32[56,512]{1,0:T(8,128)S(1)}, ...), condition=%wide.region_7.11_spmd, body=%wide.region_6.10_spmd.sunk | while | flops 6553609 | bytes 4723025 | solution.py:95
  157.3 4.3 broadcast.994
  161.6 4.2 broadcast.994.clone.1
  165.8 4.2 broadcast.994.clone.2
  170.1 196.2 %while.175 = (s32[]{:T(128)}, f32[56,512]{1,0:T(8,128)S(1)}, f32[56,512]{1,0:T(8,128)S(1)}, f32[9,8,56,512]{3,2,1,0:T(8,128)}, f32[9,8,56,512]{3,2,1,0:T(8,128)}...) while((s32[]{:T(128)}, f32[56,512]{1,0:T(8,128)S(1)}, ...), condition=%wide.region_17.21_spmd, body=%wide.region_8.20_spmd.sunk | while | flops 40468488 | bytes 15987933 | solution.py:117
  170.5 4.9 multiply_reduce_fusion.10
  192.4 4.9 multiply_reduce_fusion.10
  214.2 4.9 multiply_reduce_fusion.10
  235.9 4.9 multiply_reduce_fusion.10
  257.7 4.9 multiply_reduce_fusion.10
  279.6 4.9 multiply_reduce_fusion.10
  301.3 4.9 multiply_reduce_fusion.10
  323.1 4.9 multiply_reduce_fusion.10
  344.9 4.9 multiply_reduce_fusion.10
  366.3 32.0 %while.176 = (s32[]{:T(128)}, f32[56,512]{1,0:T(8,128)S(1)}, f32[9,8,512]{2,1,0:T(8,128)S(1)}, f32[9,8,56,512]{3,2,1,0:T(8,128)}, f32[9,8,56,512]{3,2,1,0:T(8,12...) while((s32[]{:T(128)}, f32[56,512]{1,0:T(8,128)S(1)}, ...), condition=%wide.region_28.32_spmd.clone, body=%wide.region_19.31_spmd.clone.sunk | while | flops 1114122 | bytes 4669739 | solution.py:130
  398.5 4.2 broadcast.994.clone
  402.8 30.6 %while.174 = (s32[]{:T(128)}, f32[56,512]{1,0:T(8,128)S(1)}, f32[9,8,56,512]{3,2,1,0:T(8,128)}, f32[9,8,3,56]{3,2,1,0:T(4,128)S(1)}, f32[9,8,512]{2,1,0:T(8,128)...) while((s32[]{:T(128)}, f32[56,512]{1,0:T(8,128)S(1)}, ...), condition=%wide.region_7.11_spmd, body=%wide.region_6.10_spmd.sunk | while | flops 6553609 | bytes 4723025 | solution.py:95
  433.6 4.3 broadcast.994
  437.9 4.2 broadcast.994.clone.1
  442.1 4.2 broadcast.994.clone.2
  446.4 196.2 %while.175 = (s32[]{:T(128)}, f32[56,512]{1,0:T(8,128)S(1)}, f32[56,512]{1,0:T(8,128)S(1)}, f32[9,8,56,512]{3,2,1,0:T(8,128)}, f32[9,8,56,512]{3,2,1,0:T(8,128)}...) while((s32[]{:T(128)}, f32[56,512]{1,0:T(8,128)S(1)}, ...), condition=%wide.region_17.21_spmd, body=%wide.region_8.20_spmd.sunk | while | flops 40468488 | bytes 15987933 | solution.py:117
  446.8 4.9 multiply_reduce_fusion.10
  468.7 4.9 multiply_reduce_fusion.10
  490.5 4.9 multiply_reduce_fusion.10
  512.2 4.9 multiply_reduce_fusion.10
  534.0 4.9 multiply_reduce_fusion.10
  555.8 4.9 multiply_reduce_fusion.10
  577.6 4.9 multiply_reduce_fusion.10
  599.4 4.9 multiply_reduce_fusion.10
  621.1 4.9 multiply_reduce_fusion.10
  642.5 32.0 %while.176 = (s32[]{:T(128)}, f32[56,512]{1,0:T(8,128)S(1)}, f32[9,8,512]{2,1,0:T(8,128)S(1)}, f32[9,8,56,512]{3,2,1,0:T(8,128)}, f32[9,8,56,512]{3,2,1,0:T(8,12...) while((s32[]{:T(128)}, f32[56,512]{1,0:T(8,128)S(1)}, ...), condition=%wide.region_28.32_spmd.clone, body=%wide.region_19.31_spmd.clone.sunk | while | flops 1114122 | bytes 4669739 | solution.py:130
  679.2 2.8 gather_fusion.13
  690.2 5.0 collective-permute-start.4
  695.3 3.7 collective-permute-done.4
  698.9 5.2 collective-permute-done.5
  704.5 3.9 collective-permute-start.6
  713.9 5.1 collective-permute-done.8
  719.1 3.3 collective-permute-done.9
  722.6 3.0 collective-permute-start.10
  731.4 5.4 collective-permute-done.12
  736.8 3.3 collective-permute-done.13
  (1377 shorter events, 480.3 us)
Async XLA Ops:
  7.6 50.8 %copy-start.4 = (f32[5,72,8,128]{3,2,1,0:T(8,128)S(1)}, f32[5,72,8,128]{3,2,1,0:T(8,128)}, u32[]{:S(2)}) copy-start(f32[5,72,8,128]{3,2,1,0:T(8,128)} %param.30) | copy-start | bytes 4423684
  58.3 18.1 %copy-start = (f32[72,8,128]{2,1,0:T(8,128)S(1)}, f32[72,8,128]{2,1,0:T(8,128)}, u32[]{:S(2)}) copy-start(f32[72,8,128]{2,1,0:T(8,128)} %param.31) | copy-start | bytes 884740
  58.4 20.2 %copy-start.16 = (f32[8,128]{1,0:T(8,128)S(1)}, f32[8,128]{1,0:T(8,128)}, u32[]{:S(2)}) copy-start(f32[8,128]{1,0:T(8,128)} %param.34) | copy-start | bytes 12292
  61.6 26.4 %copy-start.6 = (f32[2,72,8,128]{3,2,1,0:T(8,128)S(1)}, f32[2,72,8,128]{3,2,1,0:T(8,128)}, u32[]{:S(2)}) copy-start(f32[2,72,8,128]{3,2,1,0:T(8,128)} %param.32) | copy-start | bytes 1769476
  61.6 27.2 %copy-start.7 = (f32[8,8,1]{1,0,2:T(8,128)S(1)}, f32[8,8,1]{1,0,2:T(8,128)}, u32[]{:S(2)}) copy-start(f32[8,8,1]{1,0,2:T(8,128)} %constant.361) | copy-start | bytes 772
  72.0 36.3 %collective-permute-start.1 = (f32[5,72,512]{2,1,0:T(8,128)}, f32[5,72,512]{2,1,0:T(8,128)S(1)}, u32[]{:S(2)}, u32[]{:S(2)}) collective-permute-start(f32[5,72,512]{2,1,0:T(8,128)} %copy.78), channel_id=1, source_target_pairs={{0,64},{8,72},{16,80},{24,88},{32,96},{40,104},{48,112},{56,120},{... | collective-permute-start | bytes 2211848 | tf_op jit(solution)/shard_map/ppermute | solution.py:16
  78.6 28.2 %collective-permute-start.2 = (f32[72,512]{0,1:T(8,128)}, f32[72,512]{0,1:T(8,128)S(1)}, u32[]{:S(2)}, u32[]{:S(2)}) collective-permute-start(f32[72,512]{0,1:T(8,128)} %bitcast_select_fusion.5), channel_id=1, source_target_pairs={{0,64},{8,72},{16,80},{24,88},{32,96},{40,104},{48,112},{56,120},{... | collective-permute-start | bytes 442376 | tf_op jit(solution)/shard_map/ppermute | solution.py:16
  81.5 22.7 %collective-permute-start = (f32[2,512]{0,1:T(8,128)}, f32[2,512]{0,1:T(8,128)}, u32[]{:S(2)}, u32[]{:S(2)}) collective-permute-start(f32[2,512]{0,1:T(8,128)} %bitcast_select_fusion.7), channel_id=1, source_target_pairs={{0,64},{8,72},{16,80},{24,88},{32,96},{40,104},{48,112},{56,120},{... | collective-permute-start | bytes 12296 | tf_op jit(solution)/shard_map/ppermute | solution.py:16
  121.8 553.4 %copy-start.12 = (s32[1024]{0:T(1024)S(1)}, s32[1024]{0:T(1024)}, u32[]{:S(2)}) copy-start(s32[1024]{0:T(1024)} %get-tuple-element.1414) | copy-start | bytes 12292
  121.8 554.4 %copy-start.17 = (pred[512]{0:T(512)(128)(4,1)S(1)}, pred[512]{0:T(512)(128)(4,1)}, u32[]{:S(2)}) copy-start(pred[512]{0:T(512)(128)(4,1)} %get-tuple-element.1407) | copy-start | bytes 1540
  121.8 554.4 %copy-start.18 = (pred[512]{0:T(512)(128)(4,1)S(1)}, pred[512]{0:T(512)(128)(4,1)}, u32[]{:S(2)}) copy-start(pred[512]{0:T(512)(128)(4,1)} %get-tuple-element.1412) | copy-start | bytes 1540
  121.8 557.4 %copy-start.9 = (s32[8,128]{1,0:T(8,128)S(1)}, s32[8,128]{1,0:T(8,128)}, u32[]{:S(2)}) copy-start(s32[8,128]{1,0:T(8,128)} %param.35) | copy-start | bytes 12292
  121.8 557.4 %copy-start.11 = (s32[1024]{0:T(1024)S(1)}, s32[1024]{0:T(1024)}, u32[]{:S(2)}) copy-start(s32[1024]{0:T(1024)} %get-tuple-element.1406) | copy-start | bytes 12292
  121.9 562.8 %copy-start.10 = (s32[1024]{0:T(1024)S(1)}, s32[1024]{0:T(1024)}, u32[]{:S(2)}) copy-start(s32[1024]{0:T(1024)} %get-tuple-element.1405) | copy-start | bytes 12292
  674.8 12.6 %copy-start.13 = (pred[1024]{0:T(1024)(128)(4,1)S(1)}, pred[1024]{0:T(1024)(128)(4,1)}, u32[]{:S(2)}) copy-start(pred[1024]{0:T(1024)(128)(4,1)} %get-tuple-element.1140) | copy-start | bytes 3076
  674.8 12.6 %copy-start.14 = (pred[1024]{0:T(1024)(128)(4,1)S(1)}, pred[1024]{0:T(1024)(128)(4,1)}, u32[]{:S(2)}) copy-start(pred[1024]{0:T(1024)(128)(4,1)} %get-tuple-element.1403) | copy-start | bytes 3076
  674.9 12.6 %copy-start.15 = (pred[1024]{0:T(1024)(128)(4,1)S(1)}, pred[1024]{0:T(1024)(128)(4,1)}, u32[]{:S(2)}) copy-start(pred[1024]{0:T(1024)(128)(4,1)} %get-tuple-element.1404) | copy-start | bytes 3076
  674.9 13.7 %copy-start.1 = (f32[72,8,128]{2,1,0:T(8,128)S(1)}, f32[72,8,128]{2,1,0:T(8,128)}, u32[]{:S(2)}) copy-start(f32[72,8,128]{2,1,0:T(8,128)} %param.31) | copy-start | bytes 884740
  674.9 13.7 %copy-start.2 = (f32[1,72,8,128]{3,2,1,0:T(8,128)S(1)}, f32[1,72,8,128]{3,2,1,0:T(8,128)}, u32[]{:S(2)}) copy-start(f32[1,72,8,128]{3,2,1,0:T(8,128)} %get-tuple-element.1387) | copy-start | bytes 884740
  674.9 13.7 %copy-start.3 = (f32[1,72,8,128]{3,2,1,0:T(8,128)S(1)}, f32[1,72,8,128]{3,2,1,0:T(8,128)}, u32[]{:S(2)}) copy-start(f32[1,72,8,128]{3,2,1,0:T(8,128)} %get-tuple-element.1388) | copy-start | bytes 884740
  674.9 13.7 %copy-start.5 = (f32[128,128,1]{1,0,2:T(8,128)S(1)}, f32[128,128,1]{1,0,2:T(8,128)}, u32[]{:S(2)}) copy-start(f32[128,128,1]{1,0,2:T(8,128)} %constant.360) | copy-start | bytes 196612
  674.9 36.4 %copy-start.8 = (f32[8,8,1]{1,0,2:T(8,128)S(1)}, f32[8,8,1]{1,0,2:T(8,128)}, u32[]{:S(2)}) copy-start(f32[8,8,1]{1,0,2:T(8,128)} %constant.361) | copy-start | bytes 772
  676.5 8.2 %collective-permute-start.3 = (f32[72,512]{0,1:T(8,128)S(1)}, f32[72,512]{0,1:T(8,128)S(1)}, u32[]{:S(2)}, u32[]{:S(2)}) collective-permute-start(f32[72,512]{0,1:T(8,128)S(1)} %bitcast_select_fusion.3), channel_id=1, source_target_pairs={{0,64},{8,72},{16,80},{24,88},{32,96},{40,104},{48,112},{56,120},{... | collective-permute-start | bytes 442376 | tf_op jit(solution)/shard_map/ppermute | solution.py:16
  690.2 8.7 %collective-permute-start.4 = (f32[72,8,1]{2,0,1:T(8,128)S(1)}, f32[72,8,1]{2,0,1:T(8,128)S(1)}, u32[]{:S(2)}, u32[]{:S(2)}) collective-permute-start(f32[72,8,1]{2,0,1:T(8,128)S(1)} %get-tuple-element.1399), channel_id=1, source_target_pairs={{8,0},{16,8},{24,16},{32,24},{40,32},{48,40},{56,48},{64,56},{72,6... | collective-permute-start | bytes 6920 | tf_op jit(solution)/shard_map/ppermute | solution.py:28
  695.2 8.9 %collective-permute-start.5 = (f32[72,8,1]{2,0,1:T(8,128)S(1)}, f32[72,8,1]{2,0,1:T(8,128)S(1)}, u32[]{:S(2)}, u32[]{:S(2)}) collective-permute-start(f32[72,8,1]{2,0,1:T(8,128)S(1)} %get-tuple-element.1400), channel_id=1, source_target_pairs={{0,8},{8,16},{16,24},{24,32},{32,40},{40,48},{48,56},{56,64},{64,7... | collective-permute-start | bytes 6920 | tf_op jit(solution)/shard_map/ppermute | solution.py:25
  704.5 6.6 collective-permute-start.6
  708.4 2.7 collective-permute-start.7
  712.4 6.7 collective-permute-start.8
  712.5 9.9 %collective-permute-start.9 = (f32[72,8,1]{2,0,1:T(8,128)S(1)}, f32[72,8,1]{2,0,1:T(8,128)S(1)}, u32[]{:S(2)}, u32[]{:S(2)}) collective-permute-start(f32[72,8,1]{2,0,1:T(8,128)S(1)} %get-tuple-element.1396), channel_id=1, source_target_pairs={{0,8},{8,16},{16,24},{24,32},{32,40},{40,48},{48,56},{56,64},{64,7... | collective-permute-start | bytes 6920 | tf_op jit(solution)/shard_map/ppermute | solution.py:25
  722.6 6.0 collective-permute-start.10
  725.6 3.0 collective-permute-start.11
  729.8 7.0 collective-permute-start.12
  729.9 10.2 %collective-permute-start.13 = (f32[72,8,1]{2,0,1:T(8,128)S(1)}, f32[72,8,1]{2,0,1:T(8,128)S(1)}, u32[]{:S(2)}, u32[]{:S(2)}) collective-permute-start(f32[72,8,1]{2,0,1:T(8,128)S(1)} %get-tuple-element.1392), channel_id=1, source_target_pairs={{0,8},{8,16},{16,24},{24,32},{32,40},{40,48},{48,56},{56,64},{64,7... | collective-permute-start | bytes 6920 | tf_op jit(solution)/shard_map/ppermute | solution.py:25
  740.4 5.4 collective-permute-start.14
  743.1 2.8 collective-permute-start.15
where the time goes:
time: 753 us; the launch traced here: 747 us
  other arithmetic  459 us (61%)
  local copies, waits for them, and re-layouts  200 us (27%)
  waiting for transfers between devices  37.8 us (5%)
  starting transfers between devices  31.4 us (4%)
  loops' own time  9.14 us (1%)
    while x362, other arithmetic  238 us
    reduce_sum x18, other arithmetic, below_step(): upper_part = jnp.sum(solar_weight * (beam_now - source_here), axis=0)  88.9 us
    dynamic_update_slice x54, local copies, waits for them, and re-layouts, block_nets(): lax.scan(beam_step, jnp.broadcast_to(cosine[None, :], plane), (coeffs,) +...  61.6 us
    gather x11, local copies, waits for them, and re-layouts, local(): jnp.searchsorted(rank_end, slot_ids, side='right')  49.8 us
    another operation x13, local copies, waits for them, and re-layouts  34.2 us
    reduce_sum x18, other arithmetic, down_step(): return (diffuse_new, jnp.sum(weight * diffuse_new, axis=0))  33.1 us
    concatenate x36, other arithmetic, block_nets(): lax.scan(below_step, (ground_full, ground_full * surface_beam), (coeffs,)...  30.9 us
    add x18, other arithmetic, down_step(): diffuse_new = gain_coef * diffuse_now + offset  29.4 us
  transfers between devices with their start and end apart: 16, of which 11 were waited for; matrix products, arithmetic and copies ran while one was open for 4% of the time, Pallas kernels for 0%

commit v1 on v0

v1 whole, which is shorter than its diff:
```python
import functools

import jax
import jax.numpy as jnp
import numpy as np
from jax import lax
from jax.experimental import pallas as pl
from jax.experimental.pallas import tpu as pltpu
from jax.sharding import PartitionSpec as P

NODES = 4


TIME_INCREMENT = 0.05


def shifted(value, axis, steps):
    count = lax.axis_size(axis)
    pairs = [(source, (source + steps) % count) for source in range(count)]
    return lax.ppermute(value, axis, pairs)


def padded_2(block, sides, width):
    for axis, dim in sides:
        count = lax.axis_size(axis)
        forward = [(i, i + 1) for i in range(count - 1)]
        forward.append((count - 1, 0))
        backward = [(target, source) for source, target in forward]
        low = lax.ppermute(
            lax.slice_in_dim(block, block.shape[dim] - width, None, axis=dim), axis, forward
        )
        high = lax.ppermute(lax.slice_in_dim(block, 0, width, axis=dim), axis, backward)
        block = jnp.concatenate([low, block, high], axis=dim)
    return block


def gll_derivative():
    points = np.array([-1.0, -1.0 / np.sqrt(5.0), 1.0 / np.sqrt(5.0), 1.0])
    legendre = 0.5 * (5.0 * points**3 - 3.0 * points)
    derivative = np.zeros((4, 4))
    for source in range(4):
        for target in range(4):
            if source != target:
                derivative[source, target] = legendre[source] / (
                    legendre[target] * (points[source] - points[target])
                )
    derivative[0, 0] = -3.0
    derivative[3, 3] = 3.0
    return derivative


LOG2E = 1.4426950408889634


def coef_matrix(mol, tab):
    g, levels = mol.shape[1], mol.shape[2]
    k0, k1, k2 = mol[0].T, mol[1].T, mol[2].T
    zero = jnp.zeros_like(k0)
    full = lambda v: jnp.broadcast_to(v[None, :], k0.shape)
    lext, lalb, lasy, iext, ialb, iasy = (tab[i] for i in range(6))
    depth = jnp.stack([k0, k1, k2, full(lext), full(iext), zero, zero, zero], -1) * 2.0
    absorb = jnp.stack([k0, k1, zero, full(lext * (1 - lalb)), full(iext * (1 - ialb)), zero, zero, zero], -1)
    back = jnp.stack([zero, zero, k2, full(lext * lalb * (1 - lasy)), full(iext * ialb * (1 - iasy)), zero, zero, zero], -1)
    c = jnp.concatenate([depth, absorb, back], axis=1)
    hi = lax.reduce_precision(c, 8, 7)
    lo = c - hi
    z = jnp.zeros_like(hi)
    return jnp.concatenate([hi, hi, lo, z], axis=-1).astype(jnp.bfloat16)


def recip(x, exact):
    return pl.reciprocal(x, approx=not exact)


def rad_kernel(exact, x_ref, sfc_ref, lhs_ref, w_ref, out_ref, mm, beam, src, a_all, p_all, o_all, flux):
    levels, gtot, n = p_all.shape
    blocks = gtot // 8
    mu = sfc_ref[0:1, :]
    ground = sfc_ref[1:2, :]
    nc = jnp.broadcast_to((-0.5 * LOG2E) / mu, (8, n))

    def mults(l, slot):
        x = x_ref[l]
        hi = x.astype(jnp.bfloat16).astype(jnp.float32)
        lo = x - hi
        rhs = jnp.concatenate([hi, lo, hi, jnp.zeros_like(hi)], axis=0).astype(jnp.bfloat16)
        mm[slot] = jnp.dot(lhs_ref[l], rhs, preferred_element_type=jnp.float32)

    mults(0, 0)
    acc = jnp.zeros((8, n), jnp.float32)
    for i in range(blocks):
        sl = pl.ds(8 * i, 8)
        b0 = w_ref[sl, :n] * mu
        beam[sl, :] = b0
        src[sl, :] = jnp.zeros((8, n), jnp.float32)
        a_all[0, sl, :] = jnp.zeros((8, n), jnp.float32)
        acc = acc + b0
    flux[0:1, :] = jnp.sum(acc, axis=0, keepdims=True)

    def down(l, slot):
        acc = jnp.zeros((8, n), jnp.float32)
        for i in range(blocks):
            sl = pl.ds(8 * i, 8)
            t2 = mm[slot, sl, :]
            a = mm[slot, pl.ds(gtot + 8 * i, 8), :]
            b = mm[slot, pl.ds(2 * gtot + 8 * i, 8), :]
            bm = beam[sl, :]
            s = src[sl, :]
            alb = a_all[l, sl, :]
            c = a + b
            pr = a * c
            q = pr * lax.rsqrt(pr)
            t = jnp.tanh(q)
            u = q * (t * t)
            x = a + c
            rden = recip(t * x + (q + u), exact)
            refl = (t * b) * rden
            tran = (q - u) * rden
            bn = bm * jnp.exp2(t2 * nc)
            lost = bm - bn
            w = lost * recip(t2, exact)
            rb = w * b
            tb = lost - w * x
            inv = recip(1.0 - refl * alb, exact)
            p = tran * inv
            o = (refl * s + rb) * inv
            a1 = refl + (tran * alb) * p
            s1 = tb + p * (s + alb * rb)
            p_all[l, sl, :] = p
            o_all[l, sl, :] = o
            a_all[l + 1, sl, :] = a1
            beam[sl, :] = bn
            src[sl, :] = s1
            acc = acc + (bn + s1)
        flux[pl.ds(l + 1, 1), :] = jnp.sum(acc, axis=0, keepdims=True)

    @pl.loop(0, levels // 2)
    def _(h):
        l = 2 * h
        mults(l + 1, 1)
        down(l, 0)
        mults(jnp.minimum(l + 2, levels - 1), 0)
        down(l + 1, 1)

    us = []
    acc = jnp.zeros((8, n), jnp.float32)
    for i in range(blocks):
        sl = pl.ds(8 * i, 8)
        alb = a_all[levels, sl, :]
        up = ground * (src[sl, :] + beam[sl, :]) * (1.0 / (1.0 - ground * alb))
        us.append(up)
        acc = acc + (1.0 - alb) * up
    flux[levels:levels + 1, :] = flux[levels:levels + 1, :] - jnp.sum(acc, axis=0, keepdims=True)

    def upward(k, us):
        l = levels - 1 - k
        acc = jnp.zeros((8, n), jnp.float32)
        out = []
        for i in range(blocks):
            sl = pl.ds(8 * i, 8)
            up = p_all[l, sl, :] * us[i] + o_all[l, sl, :]
            acc = acc + (1.0 - a_all[l, sl, :]) * up
            out.append(up)
        flux[pl.ds(l, 1), :] = flux[pl.ds(l, 1), :] - jnp.sum(acc, axis=0, keepdims=True)
        return tuple(out)

    lax.fori_loop(0, levels, upward, tuple(us))
    out_ref[...] = (levels / gtot) * (flux[0:levels, :] - flux[1:levels + 1, :])


def rad(x, sfc, lhs, wb, exact=True):
    levels, _, n = x.shape
    gtot = wb.shape[0]
    f32 = jnp.float32
    return pl.pallas_call(
        functools.partial(rad_kernel, exact),
        out_shape=jax.ShapeDtypeStruct((levels, n), f32),
        in_specs=[pl.BlockSpec(memory_space=pltpu.VMEM)] * 4,
        out_specs=pl.BlockSpec(memory_space=pltpu.VMEM),
        scratch_shapes=[
            pltpu.VMEM((2, 3 * gtot, n), f32),
            pltpu.VMEM((gtot, n), f32),
            pltpu.VMEM((gtot, n), f32),
            pltpu.VMEM((levels + 1, gtot, n), f32),
            pltpu.VMEM((levels, gtot, n), f32),
            pltpu.VMEM((levels, gtot, n), f32),
            pltpu.VMEM((levels + 8, n), f32),
        ],
        compiler_params=pltpu.CompilerParams(vmem_limit_bytes=56 * 2**20),
        name="shortwave",
    )(x, sfc, lhs, wb)


def pair_average(values, before, beyond, node_index):
    return jnp.where(
        node_index == NODES - 1,
        0.5 * (values + beyond),
        jnp.where(node_index == 0, 0.5 * (before + values), values),
    )


def local(
    atmospheric_constituents,
    thermal_ratio,
    flow_velocity,
    solar_elevation_factor,
    ground_reflectivity,
    sunlit_indicator,
    molecular_optics_lookup,
    condensate_optics_lookup,
):
    levels, lines, span = thermal_ratio.shape
    half = lines // 2
    partner = lax.axis_size("gx") // 2
    low = lax.axis_index("gx") < partner
    weighted = atmospheric_constituents[2] * thermal_ratio * thermal_ratio
    state = jnp.concatenate(
        [
            (weighted * atmospheric_constituents[0])[None],
            (weighted * atmospheric_constituents[1])[None],
            atmospheric_constituents[2:],
        ],
        axis=0,
    )
    surface = jnp.stack([solar_elevation_factor, ground_reflectivity])

    def mine(value):
        return jnp.where(low, value[..., :half, :], value[..., half:, :])

    def theirs(value):
        return jnp.where(low, value[..., half:, :], value[..., :half, :])

    got_state, got_surface = shifted((theirs(state), theirs(surface)), "gx", partner)
    day_here = mine(sunlit_indicator) == 1
    work_state = jnp.where(day_here, mine(state), got_state)
    work_surface = jnp.where(day_here, mine(surface), got_surface)
    pairs = half // 2
    columns = jnp.pad(work_state, ((0, 3), (0, 0), (0, 0), (0, 0)))
    columns = columns.reshape(8, levels, 2, pairs * span).transpose(2, 1, 0, 3)
    sfc = jnp.pad(work_surface, ((0, 6), (0, 0), (0, 0))).reshape(8, 2, pairs * span).transpose(1, 0, 2)
    lhs = coef_matrix(molecular_optics_lookup, condensate_optics_lookup)
    wide = jnp.broadcast_to(
        condensate_optics_lookup[6][:, None], (condensate_optics_lookup.shape[1], pairs * span)
    )
    heats = [rad(columns[h], sfc[h], lhs, wide).reshape(levels, pairs, span) for h in range(2)]
    work_heat = jnp.concatenate(heats, axis=1)
    returned = shifted(work_heat, "gx", partner)
    both = jnp.concatenate(
        [jnp.where(low, work_heat, returned), jnp.where(low, returned, work_heat)], axis=1
    )
    radiative_warming_rate = jnp.where(sunlit_indicator == 1, both, 0.0)
    resident_span_size = span
    resident_line_number = lines
    derivative = gll_derivative()
    x_derivative = jnp.asarray(
        np.kron(np.eye(resident_span_size // NODES), derivative).T, jnp.float32
    )
    y_derivative = jnp.asarray(
        np.kron(np.eye(resident_line_number // NODES), derivative), jnp.float32
    )
    x_nodes = (jnp.arange(resident_span_size) % NODES)[None, None, :]
    y_nodes = (jnp.arange(resident_line_number) % NODES)[None, :, None]

    def averaged(values):
        padded = padded_2(values, (("gx", 2),), 1)
        along_x = pair_average(values, padded[:, :, :-2], padded[:, :, 2:], x_nodes)
        padded_y = padded_2(along_x, (("gy", 1),), 1)
        return pair_average(along_x, padded_y[:, :-2], padded_y[:, 2:], y_nodes)

    def warming_change_rate(field_now):
        slope_x = jnp.dot(
            field_now.reshape(-1, resident_span_size), x_derivative, precision=lax.Precision.HIGHEST
        ).reshape(field_now.shape)
        slope_y = jnp.einsum(
            "ij,ljx->lix", y_derivative, field_now, precision=lax.Precision.HIGHEST
        )
        return averaged(
            radiative_warming_rate - (flow_velocity[0] * slope_x + flow_velocity[1] * slope_y)
        )

    opening_advection_part = thermal_ratio + TIME_INCREMENT * warming_change_rate(thermal_ratio)
    middle_advection_part = 0.75 * thermal_ratio + 0.25 * (
        opening_advection_part + TIME_INCREMENT * warming_change_rate(opening_advection_part)
    )
    advected_thermal_ratio = 1.0 / 3.0 * thermal_ratio + 2.0 / 3.0 * (
        middle_advection_part + TIME_INCREMENT * warming_change_rate(middle_advection_part)
    )
    return (radiative_warming_rate, advected_thermal_ratio)


def solution(mesh):
    in_specs = (
        P(None, None, "gy", "gx"),
        P(None, "gy", "gx"),
        P(None, None, "gy", "gx"),
        P("gy", "gx"),
        P("gy", "gx"),
        P("gy", "gx"),
        P(),
        P(),
    )
    out_specs = (P(None, "gy", "gx"), P(None, "gy", "gx"))
    return jax.shard_map(local, mesh=mesh, in_specs=in_specs, out_specs=out_specs, check_vma=False)
```

time: 753 us -> 147 us (0.20)
  other arithmetic: 459 us -> 6.83 us
  local copies, waits for them, and re-layouts: 200 us -> 18.2 us
  Pallas kernels: 0 us -> 46.7 us
  loops' own time: 9.14 us -> 0 us
    while x362 -> x0, other arithmetic: 238 us -> none
    reduce_sum x37 -> x0, other arithmetic: 123 us -> none  [the longest x18 88.9 us: below_step(): upper_part = jnp.sum(solar_weight * (beam_now - source_here), axis=0)]
    gather x24 -> x0, local copies, waits for them, and re-layouts: 79 us -> none  [the longest x11 49.8 us: local(): jnp.searchsorted(rank_end, slot_ids, side='right')]
    dynamic_update_slice x90 -> x0, local copies, waits for them, and re-layouts: 61.9 us -> none  [the longest x54 61.6 us: block_nets(): lax.scan(beam_step, jnp.broadcast_to(cosine[None, :], plane), (coeffs,) +...]
    pallas_call x0 -> x2, Pallas kernels: none -> 46.7 us  [rad(): pl.pallas_call(functools.partial(rad_kernel, exact), out_shape=jax.ShapeD...]
    add x38 -> x0, other arithmetic: 36.3 us -> none  [the longest x18 29.4 us: down_step(): diffuse_new = gain_coef * diffuse_now + offset]
    concatenate x54 -> x2, other arithmetic: 34.3 us -> 0.73 us  [the longest x1 0.6 us: coef_matrix(): return jnp.concatenate([hi, hi, lo, z], axis=-1).astype(jnp.bfloat16)]
    another operation x14 -> x11, local copies, waits for them, and re-layouts: 34.4 us -> 1.47 us  [the longest x3 0.49 us: coef_matrix(): jnp.stack([k0, k1, k2, full(lext), full(iext), zero, zero, zero], -1) * 2.0]
  transfers between devices with their start and end apart: 16 -> 15, of which waited for: 11 -> 12; matrix products, arithmetic and copies ran while one was open for 4% -> 9% of each run, Pallas kernels for 0% -> 0%
where the time goes in v1:
time: 147 us; the launch traced here: 145 us
  Pallas kernels  46.7 us (32%)
  waiting for transfers between devices  42.6 us (29%)
  starting transfers between devices  26.7 us (18%)
  local copies, waits for them, and re-layouts  18.2 us (12%)
  other arithmetic  6.83 us (5%)
  matrix products  3.34 us (2%)
    pallas_call x2, Pallas kernels, rad(): pl.pallas_call(functools.partial(rad_kernel, exact), out_shape=jax.ShapeD...  46.7 us
    ppermute x6, waiting for transfers between devices, padded_2(): lax.ppermute(lax.slice_in_dim(block, 0, width, axis=dim), axis, backward)  20.9 us
    ppermute x6, waiting for transfers between devices, padded_2(): lax.ppermute(lax.slice_in_dim(block, block.shape[dim] - width, None, axis...  13.3 us
    ppermute x6, starting transfers between devices, padded_2(): lax.ppermute(lax.slice_in_dim(block, 0, width, axis=dim), axis, backward)  10.3 us
    ppermute x6, starting transfers between devices, padded_2(): lax.ppermute(lax.slice_in_dim(block, block.shape[dim] - width, None, axis...  9.25 us
    ppermute x3, waiting for transfers between devices, shifted(): return lax.ppermute(value, axis, pairs)  8.48 us
    ppermute x3, starting transfers between devices, shifted(): return lax.ppermute(value, axis, pairs)  7.08 us
    concatenate x2, local copies, waits for them, and re-layouts, coef_matrix(): return jnp.concatenate([hi, hi, lo, z], axis=-1).astype(jnp.bfloat16)  4.63 us
  transfers between devices with their start and end apart: 15, of which 12 were waited for; matrix products, arithmetic and copies ran while one was open for 9% of the time, Pallas kernels for 0%

profile of v1, /device:TPU:1, one launch (start us, length us, event | category | flops | bytes accessed | tf_op | source)
XLA Modules:
  0.0 145.5 jit_solution(7289227643384038745)
XLA Ops:
  0.6 1.3 fusion.66
  2.1 0.2 copy.101
  2.2 0.7 copy-done
  2.9 0.2 fusion.57
  3.3 0.9 slice_select_fusion
  4.2 4.4 %collective-permute-start = (f32[5,72,4,128]{3,1,2,0:T(8,128)}, f32[5,72,4,128]{3,1,2,0:T(8,128)}, u32[]{:S(2)}, u32[]{:S(2)}) collective-permute-start(f32[5,72,4,128]{3,1,2,0:T(8,128)} %slice_select_fusion), channel_id=1, source_target_pairs={{0,64},{8,72},{16,80},{24,88},{32,96},{40,104},{48,112},{56,120},{... | collective-permute-start | bytes 2211848 | tf_op jit(solution)/shard_map/ppermute | solution.py:20
  8.7 0.6 broadcast_select_fusion.2
  9.3 0.5 slice_bitcast_fusion.4
  9.9 0.4 stack.36
  10.4 0.9 fusion.67
  11.4 0.4 stack.37
  11.9 0.4 stack.38
  12.4 0.4 reduce-precision_convert_fusion
  12.8 0.6 maximum_maximum_fusion
  13.5 1.1 fusion.75
  14.6 0.5 select_compare_fusion
  15.1 4.6 %copy.73.lhs_ref = bf16[72,336,32]{2,1,0:T(8,128)(2,1)} copy(bf16[72,336,32]{1,2,0:T(8,128)(2,1)S(1)} %maximum_maximum_fusion) | data formatting | bytes 3096576 | tf_op jit(solution)/shard_map/concatenate | solution.py:68
  19.6 5.6 %collective-permute-done.1 = f32[2,4,128]{2,1,0:T(4,128)} collective-permute-done((f32[2,4,128]{2,1,0:T(4,128)}, f32[2,4,128]{2,1,0:T(4,128)}, u32[]{:S(2)}, u32[]{:S(2)}) %collective-permute-start.1) | collective-permute-done | bytes 4128 | tf_op jit(solution)/shard_map/ppermute | solution.py:20
  25.3 0.7 select_select_fusion.1
  26.0 0.6 slice_bitcast_fusion.2
  26.6 1.2 select_select_fusion
  27.8 0.2 copy.104
  28.0 0.2 pad.8.clone
  28.2 1.0 reshape.71
  29.2 0.7 copy.159
  29.9 1.1 slice_bitcast_fusion
  31.0 0.7 broadcast_in_dim.111.w_ref
  31.8 23.3 %shortwave.2 = f32[72,256]{1,0:T(8,128)} custom-call(f32[72,8,256]{2,1,0:T(8,128)} %get-tuple-element.12.x_ref, f32[8,256]{1,0:T(8,128)} %get-tuple-element.37.sfc_ref, bf16[72,336,32]{2,1,0:T(8,128)(2,1)} %copy.73.lhs_ref, f32[112,256]{1,0:T(8,128)} %broadcast_in_dim.111.w_ref), custom_call_target="tpu_custom_call" | custom-call | tf_op jit(solution)/shard_map/shortwave/pallas_call | solution.py:175
  55.1 0.9 bitcast_dynamic-update-slice_fusion.1
  56.0 23.4 %shortwave.3 = f32[72,256]{1,0:T(8,128)} custom-call(f32[72,8,256]{2,1,0:T(8,128)} %get-tuple-element.11.x_ref, f32[8,256]{1,0:T(8,128)} %get-tuple-element.36.sfc_ref, bf16[72,336,32]{2,1,0:T(8,128)(2,1)} %copy.73.lhs_ref, f32[112,256]{1,0:T(8,128)} %broadcast_in_dim.111.w_ref), custom_call_target="tpu_custom_call" | custom-call | tf_op jit(solution)/shard_map/shortwave/pallas_call | solution.py:175
  79.4 0.9 bitcast_dynamic-update-slice_fusion
  80.3 2.6 %collective-permute-start.2 = (f32[72,4,128]{2,0,1:T(8,128)S(1)}, f32[72,4,128]{2,0,1:T(8,128)S(1)}, u32[]{:S(2)}, u32[]{:S(2)}) collective-permute-start(f32[72,4,128]{2,0,1:T(8,128)S(1)} %bitcast_dynamic-update-slice_fusion), channel_id=1, source_target_pairs={{0,64},{8,72},{16,80},{24,88},{32,96},{40,104},{48,112},{56,120},{... | collective-permute-start | bytes 442376 | tf_op jit(solution)/shard_map/ppermute | solution.py:20
  82.9 2.8 %collective-permute-done.2 = f32[72,4,128]{2,0,1:T(8,128)S(1)} collective-permute-done((f32[72,4,128]{2,0,1:T(8,128)S(1)}, f32[72,4,128]{2,0,1:T(8,128)S(1)}, u32[]{:S(2)}, u32[]{:S(2)}) %collective-permute-start.2) | collective-permute-done | bytes 147488 | tf_op jit(solution)/shard_map/ppermute | solution.py:20
  85.9 0.5 fusion.6
  86.5 5.3 %collective-permute-start.3 = (f32[72,8,1]{2,0,1:T(8,128)S(1)}, f32[72,8,1]{2,0,1:T(8,128)S(1)}, u32[]{:S(2)}, u32[]{:S(2)}) collective-permute-start(f32[72,8,1]{2,0,1:T(8,128)S(1)} %get-tuple-element.29), channel_id=1, source_target_pairs={{8,0},{16,8},{24,16},{32,24},{40,32},{48,40},{56,48},{64,56},{72,6... | collective-permute-start | bytes 6920 | tf_op jit(solution)/shard_map/ppermute | solution.py:32
  91.8 3.7 %collective-permute-done.3 = f32[72,8,1]{2,0,1:T(8,128)S(1)} collective-permute-done((f32[72,8,1]{2,0,1:T(8,128)S(1)}, f32[72,8,1]{2,0,1:T(8,128)S(1)}, u32[]{:S(2)}, u32[]{:S(2)}) %collective-permute-start.3) | collective-permute-done | bytes 2336 | tf_op jit(solution)/shard_map/ppermute | solution.py:32
  95.5 5.2 %collective-permute-done.4 = f32[72,8,1]{2,0,1:T(8,128)S(1)} collective-permute-done((f32[72,8,1]{2,0,1:T(8,128)S(1)}, f32[72,8,1]{2,0,1:T(8,128)S(1)}, u32[]{:S(2)}, u32[]{:S(2)}) %collective-permute-start.4) | collective-permute-done | bytes 2336 | tf_op jit(solution)/shard_map/ppermute | solution.py:29
  100.7 0.3 fusion.51
  101.0 4.2 %collective-permute-start.5 = (f32[72,1,128]{2,0,1:T(8,128)S(1)}, f32[72,1,128]{2,0,1:T(8,128)S(1)}, u32[]{:S(2)}, u32[]{:S(2)}) collective-permute-start(f32[72,1,128]{2,0,1:T(8,128)S(1)} %get-tuple-element.27), channel_id=1, source_target_pairs={{1,0},{2,1},{3,2},{4,3},{5,4},{6,5},{7,6},{0,7},{9,8},{10,9},{11,1... | collective-permute-start | bytes 110600 | tf_op jit(solution)/shard_map/ppermute | solution.py:32
  105.2 1.1 collective-permute-start.6
  106.3 1.6 %collective-permute-done.5 = f32[72,1,128]{2,0,1:T(8,128)S(1)} collective-permute-done((f32[72,1,128]{2,0,1:T(8,128)S(1)}, f32[72,1,128]{2,0,1:T(8,128)S(1)}, u32[]{:S(2)}, u32[]{:S(2)}) %collective-permute-start.5) | collective-permute-done | bytes 36896 | tf_op jit(solution)/shard_map/ppermute | solution.py:32
  107.9 0.2 fusion.45
  108.1 0.4 fusion.60
  108.5 0.5 fusion.2
  109.3 1.5 collective-permute-start.8
  110.7 5.2 %collective-permute-done.7 = f32[72,8,1]{2,0,1:T(8,128)S(1)} collective-permute-done((f32[72,8,1]{2,0,1:T(8,128)S(1)}, f32[72,8,1]{2,0,1:T(8,128)S(1)}, u32[]{:S(2)}, u32[]{:S(2)}) %collective-permute-start.7) | collective-permute-done | bytes 2336 | tf_op jit(solution)/shard_map/ppermute | solution.py:32
  115.9 3.6 %collective-permute-done.8 = f32[72,8,1]{2,0,1:T(8,128)S(1)} collective-permute-done((f32[72,8,1]{2,0,1:T(8,128)S(1)}, f32[72,8,1]{2,0,1:T(8,128)S(1)}, u32[]{:S(2)}, u32[]{:S(2)}) %collective-permute-start.8) | collective-permute-done | bytes 2336 | tf_op jit(solution)/shard_map/ppermute | solution.py:29
  119.5 0.3 fusion.37
  119.8 4.2 %collective-permute-start.10 = (f32[72,1,128]{2,0,1:T(8,128)S(1)}, f32[72,1,128]{2,0,1:T(8,128)S(1)}, u32[]{:S(2)}, u32[]{:S(2)}) collective-permute-start(f32[72,1,128]{2,0,1:T(8,128)S(1)} %get-tuple-element.24), channel_id=1, source_target_pairs={{0,1},{1,2},{2,3},{3,4},{4,5},{5,6},{6,7},{7,0},{8,9},{9,10},{10,1... | collective-permute-start | bytes 110600 | tf_op jit(solution)/shard_map/ppermute | solution.py:29
  124.0 1.1 collective-permute-done.10
  125.0 2.3 %collective-permute-done.9 = f32[72,1,128]{2,0,1:T(8,128)S(1)} collective-permute-done((f32[72,1,128]{2,0,1:T(8,128)S(1)}, f32[72,1,128]{2,0,1:T(8,128)S(1)}, u32[]{:S(2)}, u32[]{:S(2)}) %collective-permute-start.9) | collective-permute-done | bytes 36896 | tf_op jit(solution)/shard_map/ppermute | solution.py:32
  127.3 0.2 fusion.31
  127.5 0.4 fusion.58
  127.9 0.5 fusion.3
  128.7 1.5 collective-permute-start.12
  130.1 7.3 %collective-permute-done.11 = f32[72,8,1]{2,0,1:T(8,128)S(1)} collective-permute-done((f32[72,8,1]{2,0,1:T(8,128)S(1)}, f32[72,8,1]{2,0,1:T(8,128)S(1)}, u32[]{:S(2)}, u32[]{:S(2)}) %collective-permute-start.11) | collective-permute-done | bytes 2336 | tf_op jit(solution)/shard_map/ppermute | solution.py:32
  137.4 3.4 %collective-permute-done.12 = f32[72,8,1]{2,0,1:T(8,128)S(1)} collective-permute-done((f32[72,8,1]{2,0,1:T(8,128)S(1)}, f32[72,8,1]{2,0,1:T(8,128)S(1)}, u32[]{:S(2)}, u32[]{:S(2)}) %collective-permute-start.12) | collective-permute-done | bytes 2336 | tf_op jit(solution)/shard_map/ppermute | solution.py:29
  140.8 0.3 fusion.21
  141.1 0.7 collective-permute-start.13
  141.8 1.0 collective-permute-start.14
  142.8 0.8 copy.92
  143.6 0.9 collective-permute-done.13
  144.5 0.2 fusion.15
  144.7 0.8 copy.93
  (63 shorter events, 1.4 us)
Async XLA Ops:
  0.6 1.4 slice-start
  1.9 1.0 copy-start
  3.2 5.4 %copy-start.8 = (f32[8,128]{1,0:T(8,128)S(1)}, f32[8,128]{1,0:T(8,128)}, u32[]{:S(2)}) copy-start(f32[8,128]{1,0:T(8,128)} %param.14) | copy-start | bytes 12292
  3.2 5.4 %copy-start.9 = (f32[8,128]{1,0:T(8,128)S(1)}, f32[8,128]{1,0:T(8,128)}, u32[]{:S(2)}) copy-start(f32[8,128]{1,0:T(8,128)} %param.13) | copy-start | bytes 12292
  3.2 6.0 %copy-start.11 = (f32[7,112]{1,0:T(8,128)S(1)}, f32[7,112]{1,0:T(8,128)}, u32[]{:S(2)}) copy-start(f32[7,112]{1,0:T(8,128)} %param.17) | copy-start | bytes 9412
  3.3 6.5 %copy-start.6 = (f32[3,112,72]{1,2,0:T(8,128)S(1)}, f32[3,112,72]{1,2,0:T(8,128)}, u32[]{:S(2)}) copy-start(f32[3,112,72]{1,2,0:T(8,128)} %param.16) | copy-start | bytes 290308
  3.3 7.2 %copy-start.5 = (f32[2,72,8,128]{3,2,1,0:T(8,128)S(1)}, f32[2,72,8,128]{3,2,1,0:T(8,128)}, u32[]{:S(2)}) copy-start(f32[2,72,8,128]{3,2,1,0:T(8,128)} %param.12) | copy-start | bytes 1769476
  4.2 22.4 %collective-permute-start = (f32[5,72,4,128]{3,1,2,0:T(8,128)}, f32[5,72,4,128]{3,1,2,0:T(8,128)}, u32[]{:S(2)}, u32[]{:S(2)}) collective-permute-start(f32[5,72,4,128]{3,1,2,0:T(8,128)} %slice_select_fusion), channel_id=1, source_target_pairs={{0,64},{8,72},{16,80},{24,88},{32,96},{40,104},{48,112},{56,120},{... | collective-permute-start | bytes 2211848 | tf_op jit(solution)/shard_map/ppermute | solution.py:20
  9.3 16.0 %collective-permute-start.1 = (f32[2,4,128]{2,1,0:T(4,128)}, f32[2,4,128]{2,1,0:T(4,128)}, u32[]{:S(2)}, u32[]{:S(2)}) collective-permute-start(f32[2,4,128]{2,1,0:T(4,128)} %broadcast_select_fusion.2), channel_id=1, source_target_pairs={{0,64},{8,72},{16,80},{24,88},{32,96},{40,104},{48,112},{56,120},{... | collective-permute-start | bytes 12296 | tf_op jit(solution)/shard_map/ppermute | solution.py:20
  12.8 0.7 copy-start.7
  12.8 1.8 %copy-start.10 = (s32[8,128]{1,0:T(8,128)S(1)}, s32[8,128]{1,0:T(8,128)}, u32[]{:S(2)}) copy-start(s32[8,128]{1,0:T(8,128)} %param.15) | copy-start | bytes 12292
  29.9 1.1 copy-start.12
  56.0 29.9 %copy-start.1 = (f32[1,72,8,128]{3,2,1,0:T(8,128)S(1)}, f32[1,72,8,128]{3,2,1,0:T(8,128)}, u32[]{:S(2)}) copy-start(f32[1,72,8,128]{3,2,1,0:T(8,128)} %get-tuple-element.15) | copy-start | bytes 884740
  56.0 29.9 %copy-start.2 = (f32[1,72,8,128]{3,2,1,0:T(8,128)S(1)}, f32[1,72,8,128]{3,2,1,0:T(8,128)}, u32[]{:S(2)}) copy-start(f32[1,72,8,128]{3,2,1,0:T(8,128)} %get-tuple-element.16) | copy-start | bytes 884740
  56.0 29.9 %copy-start.3 = (f32[8,72,128]{2,0,1:T(8,128)S(1)}, f32[8,72,128]{2,0,1:T(8,128)}, u32[]{:S(2)}) copy-start(f32[8,72,128]{2,0,1:T(8,128)} %fusion.75) | copy-start | bytes 884740
  56.0 29.9 %copy-start.4 = (f32[128,128,1]{1,0,2:T(8,128)S(1)}, f32[128,128,1]{1,0,2:T(8,128)}, u32[]{:S(2)}) copy-start(f32[128,128,1]{1,0,2:T(8,128)} %constant.75) | copy-start | bytes 196612
  80.3 5.5 %collective-permute-start.2 = (f32[72,4,128]{2,0,1:T(8,128)S(1)}, f32[72,4,128]{2,0,1:T(8,128)S(1)}, u32[]{:S(2)}, u32[]{:S(2)}) collective-permute-start(f32[72,4,128]{2,0,1:T(8,128)S(1)} %bitcast_dynamic-update-slice_fusion), channel_id=1, source_target_pairs={{0,64},{8,72},{16,80},{24,88},{32,96},{40,104},{48,112},{56,120},{... | collective-permute-start | bytes 442376 | tf_op jit(solution)/shard_map/ppermute | solution.py:20
  86.5 9.0 %collective-permute-start.3 = (f32[72,8,1]{2,0,1:T(8,128)S(1)}, f32[72,8,1]{2,0,1:T(8,128)S(1)}, u32[]{:S(2)}, u32[]{:S(2)}) collective-permute-start(f32[72,8,1]{2,0,1:T(8,128)S(1)} %get-tuple-element.29), channel_id=1, source_target_pairs={{8,0},{16,8},{24,16},{32,24},{40,32},{48,40},{56,48},{64,56},{72,6... | collective-permute-start | bytes 6920 | tf_op jit(solution)/shard_map/ppermute | solution.py:32
  91.8 8.9 %collective-permute-start.4 = (f32[72,8,1]{2,0,1:T(8,128)S(1)}, f32[72,8,1]{2,0,1:T(8,128)S(1)}, u32[]{:S(2)}, u32[]{:S(2)}) collective-permute-start(f32[72,8,1]{2,0,1:T(8,128)S(1)} %get-tuple-element.30), channel_id=1, source_target_pairs={{0,8},{8,16},{16,24},{24,32},{32,40},{40,48},{48,56},{56,64},{64,7... | collective-permute-start | bytes 6920 | tf_op jit(solution)/shard_map/ppermute | solution.py:29
  101.0 6.9 %collective-permute-start.5 = (f32[72,1,128]{2,0,1:T(8,128)S(1)}, f32[72,1,128]{2,0,1:T(8,128)S(1)}, u32[]{:S(2)}, u32[]{:S(2)}) collective-permute-start(f32[72,1,128]{2,0,1:T(8,128)S(1)} %get-tuple-element.27), channel_id=1, source_target_pairs={{1,0},{2,1},{3,2},{4,3},{5,4},{6,5},{7,6},{0,7},{9,8},{10,9},{11,1... | collective-permute-start | bytes 110600 | tf_op jit(solution)/shard_map/ppermute | solution.py:32
  105.2 2.7 %collective-permute-start.6 = (f32[72,1,128]{2,0,1:T(8,128)S(1)}, f32[72,1,128]{2,0,1:T(8,128)S(1)}, u32[]{:S(2)}, u32[]{:S(2)}) collective-permute-start(f32[72,1,128]{2,0,1:T(8,128)S(1)} %get-tuple-element.28), channel_id=1, source_target_pairs={{0,1},{1,2},{2,3},{3,4},{4,5},{5,6},{6,7},{7,0},{8,9},{9,10},{10,1... | collective-permute-start | bytes 110600 | tf_op jit(solution)/shard_map/ppermute | solution.py:29
  109.2 6.7 %collective-permute-start.7 = (f32[72,8,1]{2,0,1:T(8,128)S(1)}, f32[72,8,1]{2,0,1:T(8,128)S(1)}, u32[]{:S(2)}, u32[]{:S(2)}) collective-permute-start(f32[72,8,1]{2,0,1:T(8,128)S(1)} %get-tuple-element.25), channel_id=1, source_target_pairs={{8,0},{16,8},{24,16},{32,24},{40,32},{48,40},{56,48},{64,56},{72,6... | collective-permute-start | bytes 6920 | tf_op jit(solution)/shard_map/ppermute | solution.py:32
  109.3 10.2 %collective-permute-start.8 = (f32[72,8,1]{2,0,1:T(8,128)S(1)}, f32[72,8,1]{2,0,1:T(8,128)S(1)}, u32[]{:S(2)}, u32[]{:S(2)}) collective-permute-start(f32[72,8,1]{2,0,1:T(8,128)S(1)} %get-tuple-element.26), channel_id=1, source_target_pairs={{0,8},{8,16},{16,24},{24,32},{32,40},{40,48},{48,56},{56,64},{64,7... | collective-permute-start | bytes 6920 | tf_op jit(solution)/shard_map/ppermute | solution.py:29
  119.8 5.2 %collective-permute-start.10 = (f32[72,1,128]{2,0,1:T(8,128)S(1)}, f32[72,1,128]{2,0,1:T(8,128)S(1)}, u32[]{:S(2)}, u32[]{:S(2)}) collective-permute-start(f32[72,1,128]{2,0,1:T(8,128)S(1)} %get-tuple-element.24), channel_id=1, source_target_pairs={{0,1},{1,2},{2,3},{3,4},{4,5},{5,6},{6,7},{7,0},{8,9},{9,10},{10,1... | collective-permute-start | bytes 110600 | tf_op jit(solution)/shard_map/ppermute | solution.py:29
  123.9 3.4 %collective-permute-start.9 = (f32[72,1,128]{2,0,1:T(8,128)S(1)}, f32[72,1,128]{2,0,1:T(8,128)S(1)}, u32[]{:S(2)}, u32[]{:S(2)}) collective-permute-start(f32[72,1,128]{2,0,1:T(8,128)S(1)} %get-tuple-element.23), channel_id=1, source_target_pairs={{1,0},{2,1},{3,2},{4,3},{5,4},{6,5},{7,6},{0,7},{9,8},{10,9},{11,1... | collective-permute-start | bytes 110600 | tf_op jit(solution)/shard_map/ppermute | solution.py:32
  128.6 8.8 %collective-permute-start.11 = (f32[72,8,1]{2,0,1:T(8,128)S(1)}, f32[72,8,1]{2,0,1:T(8,128)S(1)}, u32[]{:S(2)}, u32[]{:S(2)}) collective-permute-start(f32[72,8,1]{2,0,1:T(8,128)S(1)} %get-tuple-element.21), channel_id=1, source_target_pairs={{8,0},{16,8},{24,16},{32,24},{40,32},{48,40},{56,48},{64,56},{72,6... | collective-permute-start | bytes 6920 | tf_op jit(solution)/shard_map/ppermute | solution.py:32
  128.7 12.1 %collective-permute-start.12 = (f32[72,8,1]{2,0,1:T(8,128)S(1)}, f32[72,8,1]{2,0,1:T(8,128)S(1)}, u32[]{:S(2)}, u32[]{:S(2)}) collective-permute-start(f32[72,8,1]{2,0,1:T(8,128)S(1)} %get-tuple-element.22), channel_id=1, source_target_pairs={{0,8},{8,16},{16,24},{24,32},{32,40},{40,48},{48,56},{56,64},{64,7... | collective-permute-start | bytes 6920 | tf_op jit(solution)/shard_map/ppermute | solution.py:29
  141.1 3.4 %collective-permute-start.13 = (f32[72,1,128]{2,0,1:T(8,128)S(1)}, f32[72,1,128]{2,0,1:T(8,128)S(1)}, u32[]{:S(2)}, u32[]{:S(2)}) collective-permute-start(f32[72,1,128]{2,0,1:T(8,128)S(1)} %get-tuple-element.19), channel_id=1, source_target_pairs={{1,0},{2,1},{3,2},{4,3},{5,4},{6,5},{7,6},{0,7},{9,8},{10,9},{11,1... | collective-permute-start | bytes 110600 | tf_op jit(solution)/shard_map/ppermute | solution.py:32
  141.8 2.7 %collective-permute-start.14 = (f32[72,1,128]{2,0,1:T(8,128)S(1)}, f32[72,1,128]{2,0,1:T(8,128)S(1)}, u32[]{:S(2)}, u32[]{:S(2)}) collective-permute-start(f32[72,1,128]{2,0,1:T(8,128)S(1)} %get-tuple-element.20), channel_id=1, source_target_pairs={{0,1},{1,2},{2,3},{3,4},{4,5},{5,6},{6,7},{7,0},{8,9},{9,10},{10,1... | collective-permute-start | bytes 110600 | tf_op jit(solution)/shard_map/ppermute | solution.py:29

commit v2 on v1

v2 whole, which is shorter than its diff:
```python
import functools

import jax
import jax.numpy as jnp
import numpy as np
from jax import lax
from jax.experimental import pallas as pl
from jax.experimental.pallas import tpu as pltpu
from jax.sharding import PartitionSpec as P

NODES = 4
TIME_INCREMENT = 0.05
LOG2E = 1.4426950408889634
MESH = pl.DeviceIdType.MESH
FIELDS = 5
PACK = 4


def gll_derivative():
    points = np.array([-1.0, -1.0 / np.sqrt(5.0), 1.0 / np.sqrt(5.0), 1.0])
    legendre = 0.5 * (5.0 * points**3 - 3.0 * points)
    derivative = np.zeros((4, 4))
    for source in range(4):
        for target in range(4):
            if source != target:
                derivative[source, target] = legendre[source] / (
                    legendre[target] * (points[source] - points[target])
                )
    derivative[0, 0] = -3.0
    derivative[3, 3] = 3.0
    return derivative


def coef_matrix(mol, tab):
    k0, k1, k2 = mol[0].T, mol[1].T, mol[2].T
    levels, gpoints = k0.shape
    zero = jnp.zeros_like(k0)
    lext, lalb, lasy, iext, ialb, iasy = (
        jnp.broadcast_to(tab[i][None, :], k0.shape) for i in range(6)
    )
    pad = [zero] * 3
    depth = jnp.stack([2 * k0, 2 * k1, 2 * k2, 2 * lext, 2 * iext] + pad, -1)
    absorb = jnp.stack([k0, k1, zero, lext * (1 - lalb), iext * (1 - ialb)] + pad, -1)
    back = jnp.stack(
        [zero, zero, k2, lext * lalb * (1 - lasy), iext * ialb * (1 - iasy)] + pad, -1
    )
    coefs = jnp.concatenate([depth, absorb, back], axis=1)
    high = lax.reduce_precision(coefs, 8, 7)
    low = coefs - high
    wide = jnp.concatenate([high, high, low, jnp.zeros_like(high)], axis=-1)
    wide = wide.reshape(levels // PACK, PACK, 3 * gpoints, 32).transpose(0, 2, 1, 3)
    return wide.reshape(levels // PACK, 3 * gpoints, PACK * 32).astype(jnp.bfloat16)


def shortwave(x_ref, mu, ground, lhs_ref, w_ref, out_ref, mm, beam, src, a_all, p_all, o_all, flux):
    levels, gtot, n = p_all.shape
    blocks = gtot // 8
    f32 = jnp.float32
    nc = jnp.broadcast_to((-0.5 * LOG2E) / mu, (8, n))

    def mults(l, slot):
        x = jnp.concatenate(
            [x_ref[r, pl.ds(l, 8, stride=levels), :] for r in range(x_ref.shape[0])], axis=1
        )
        high = x.astype(jnp.bfloat16).astype(f32)
        low = x - high
        nil = jnp.zeros_like(high)
        inner = lax.rem(l, PACK)
        parts = []
        for j in range(PACK):
            hit = inner == j
            h = jnp.where(hit, high, nil)
            parts += [h, jnp.where(hit, low, nil), h, nil]
        rhs = jnp.concatenate(parts, axis=0).astype(jnp.bfloat16)
        mm[slot] = jnp.dot(lhs_ref[l // PACK], rhs, preferred_element_type=f32)

    mults(0, 0)
    acc = jnp.zeros((8, n), f32)
    for i in range(blocks):
        sl = pl.ds(8 * i, 8)
        first = w_ref[sl, :] * mu
        beam[sl, :] = first
        src[sl, :] = jnp.zeros((8, n), f32)
        a_all[0, sl, :] = jnp.zeros((8, n), f32)
        acc = acc + first
    flux[0:1, :] = jnp.sum(acc, axis=0, keepdims=True)

    def down(l, slot):
        acc = jnp.zeros((8, n), f32)
        for i in range(blocks):
            sl = pl.ds(8 * i, 8)
            t2 = mm[slot, sl, :]
            a = mm[slot, pl.ds(gtot + 8 * i, 8), :]
            b = mm[slot, pl.ds(2 * gtot + 8 * i, 8), :]
            bm = beam[sl, :]
            s = src[sl, :]
            alb = a_all[l, sl, :]
            c = a + b
            pr = a * c
            q = pr * lax.rsqrt(pr)
            t = jnp.tanh(q)
            u = q * (t * t)
            x = a + c
            rden = 1.0 / (t * x + (q + u))
            refl = (t * b) * rden
            tran = (q - u) * rden
            bn = bm * jnp.exp2(t2 * nc)
            lost = bm - bn
            w = lost * (1.0 / t2)
            rb = w * b
            tb = lost - w * x
            inv = 1.0 / (1.0 - refl * alb)
            p = tran * inv
            o = (refl * s + rb) * inv
            a1 = refl + (tran * alb) * p
            s1 = tb + p * (s + alb * rb)
            p_all[l, sl, :] = p
            o_all[l, sl, :] = o
            a_all[l + 1, sl, :] = a1
            beam[sl, :] = bn
            src[sl, :] = s1
            acc = acc + (bn + s1)
        flux[pl.ds(l + 1, 1), :] = jnp.sum(acc, axis=0, keepdims=True)

    @pl.loop(0, levels // 2)
    def _(h):
        l = 2 * h
        mults(l + 1, 1)
        down(l, 0)
        mults(jnp.minimum(l + 2, levels - 1), 0)
        down(l + 1, 1)

    ups = []
    acc = jnp.zeros((8, n), f32)
    for i in range(blocks):
        sl = pl.ds(8 * i, 8)
        alb = a_all[levels, sl, :]
        up = ground * (src[sl, :] + beam[sl, :]) * (1.0 / (1.0 - ground * alb))
        ups.append(up)
        acc = acc + (1.0 - alb) * up
    last = pl.ds(levels, 1)
    flux[last, :] = flux[last, :] - jnp.sum(acc, axis=0, keepdims=True)

    def upward(k, ups):
        l = levels - 1 - k
        acc = jnp.zeros((8, n), f32)
        out = []
        for i in range(blocks):
            sl = pl.ds(8 * i, 8)
            up = p_all[l, sl, :] * ups[i] + o_all[l, sl, :]
            acc = acc + (1.0 - a_all[l, sl, :]) * up
            out.append(up)
        row = pl.ds(l, 1)
        flux[row, :] = flux[row, :] - jnp.sum(acc, axis=0, keepdims=True)
        return tuple(out)

    lax.fori_loop(0, levels, upward, tuple(ups))
    out_ref[...] = (levels / gtot) * (flux[0:levels, :] - flux[1 : levels + 1, :])


def whole_kernel(
    nx, ny, state_ref, temp_ref, flow_ref, mu_ref, ground_ref, day_ref, lhs_ref, w_ref,
    heat_ref, adv_ref,
    snd, got, xs, mm, beam, src, a_all, p_all, o_all, flux, hwork, hgot,
    raw, cur, rowsnd, rowgot, edgesnd, edgegot,
    state_send, state_recv, heat_send, heat_recv, halo_send, halo_recv,
):
    f32 = jnp.float32
    gx, gy = lax.axis_index("gx"), lax.axis_index("gy")
    lines, span = mu_ref.shape
    total = temp_ref.shape[0]
    levels = total // lines
    half = lines // 2
    pair = half // 2
    east, west = lax.rem(gx + 1, nx), lax.rem(gx + nx - 1, nx)
    south, north = lax.rem(gy + 1, ny), lax.rem(gy + ny - 1, ny)
    far = lax.rem(gx + nx // 2, nx)
    mine = jnp.where(gx < nx // 2, 0, half)
    theirs = half - mine

    targets = [
        (east, gy), (east, south), (east, north),
        (west, gy), (west, south), (west, north),
        (gx, south), (gx, north),
    ]
    barrier = pltpu.get_barrier_semaphore()
    for device in targets + [(far, gy)]:
        pl.semaphore_signal(barrier, inc=1, device_id=device, device_id_type=MESH)
    pl.semaphore_wait(barrier, len(targets) + 1)

    def products(line, store):
        line_of = lambda ref, k: ref[pl.ds(k * total + line, levels, stride=lines), :]
        temper = line_of(temp_ref, 0)
        thick = line_of(state_ref, 2)
        weighted = thick * temper * temper
        values = [
            weighted * line_of(state_ref, 0),
            weighted * line_of(state_ref, 1),
            thick,
            line_of(state_ref, 3),
            line_of(state_ref, 4),
        ]
        for k, value in enumerate(values):
            store(slice(k * levels, (k + 1) * levels), value)

    def state_copy(h):
        return pltpu.make_async_remote_copy(
            src_ref=snd.at[h], dst_ref=got.at[h], send_sem=state_send.at[h],
            recv_sem=state_recv.at[h], device_id=(far, gy), device_id_type=MESH,
        )

    def heat_copy(h):
        return pltpu.make_async_remote_copy(
            src_ref=hwork.at[h], dst_ref=hgot.at[h], send_sem=heat_send.at[h],
            recv_sem=heat_recv.at[h], device_id=(far, gy), device_id_type=MESH,
        )

    tail = FIELDS * levels
    for h in range(2):
        for r in range(pair):
            lanes = slice(r * span, (r + 1) * span)
            line = theirs + pair * h + r

            def to_send(rows, value, h=h, lanes=lanes):
                snd[h, rows, lanes] = value

            products(line, to_send)
            snd[h, tail : tail + 1, lanes] = mu_ref[pl.ds(line, 1), :]
            snd[h, tail + 1 : tail + 2, lanes] = ground_ref[pl.ds(line, 1), :]
            snd[h, tail + 2 : tail + 8, lanes] = jnp.zeros((6, span), f32)
        state_copy(h).start()

    for h in range(2):
        for r in range(pair):
            xs[h, r, tail:, :] = jnp.zeros((xs.shape[2] - tail, span), f32)

            def to_own(rows, value, h=h, r=r):
                xs[h, r, rows, :] = value

            products(mine + pair * h + r, to_own)

    dref = gll_derivative()
    lane = lax.broadcasted_iota(jnp.int32, (lines, span), 1)
    line_no = lax.broadcasted_iota(jnp.int32, (lines, span), 0)
    node_x, node_y = lane % NODES, line_no % NODES

    def taps(node):
        out = []
        for k in range(1 - NODES, NODES):
            coef = jnp.zeros((lines, span), f32)
            for i in range(NODES):
                if 0 <= i + k < NODES and dref[i, i + k] != 0.0:
                    coef = jnp.where(node == i, float(dref[i, i + k]), coef)
            out.append((k, coef))
        return out

    taps_x, taps_y = taps(node_x), taps(node_y)

    def slope(v, axis, size, table):
        out = None
        for k, coef in table:
            moved = v if k == 0 else pltpu.roll(v, (-k) % size, axis)
            out = coef * moved if out is None else out + coef * moved
        return out

    def at(l):
        return pl.ds(pl.multiple_of(l * lines, lines), lines)

    def wind(v, l):
        return flow_ref[at(l), :] * slope(v, 1, span, taps_x) + flow_ref[
            at(levels + l), :
        ] * slope(v, 0, lines, taps_y)

    group = 8

    @pl.loop(0, levels // group)
    def _(j):
        for i in range(group):
            l = j * group + i
            raw[at(l), :] = wind(temp_ref[at(l), :], l)

    for h in range(2):
        state_copy(h).wait_recv()
        mus, grounds = [], []
        for r in range(pair):
            lanes = slice(r * span, (r + 1) * span)
            line = pl.ds(mine + pair * h + r, 1)
            own = day_ref[line, :] == 1
            for k in range(FIELDS):
                rows = slice(k * levels, (k + 1) * levels)
                xs[h, r, rows, :] = jnp.where(own, xs[h, r, rows, :], got[h, rows, lanes])
            mus.append(jnp.where(own, mu_ref[line, :], got[h, tail : tail + 1, lanes]))
            grounds.append(jnp.where(own, ground_ref[line, :], got[h, tail + 1 : tail + 2, lanes]))
        shortwave(
            xs.at[h], jnp.concatenate(mus, axis=1), jnp.concatenate(grounds, axis=1),
            lhs_ref, w_ref, hwork.at[h], mm, beam, src, a_all, p_all, o_all, flux,
        )
        heat_copy(h).start()

    def place(source, first, h):
        for r in range(pair):
            line = first + pair * h + r
            own = day_ref[pl.ds(line, 1), :] == 1
            heat_ref[pl.ds(line, levels, stride=lines), :] = jnp.where(
                own, source[h, :, r * span : (r + 1) * span], 0.0
            )

    for h in range(2):
        place(hwork, mine, h)
    for h in range(2):
        heat_copy(h).wait_recv()
        place(hgot, theirs, h)

    def average(v, before, beyond, node):
        return jnp.where(
            node == NODES - 1, 0.5 * (v + beyond), jnp.where(node == 0, 0.5 * (before + v), v)
        )

    def average_y(v, above, under):
        before = jnp.where(line_no == 0, above, pltpu.roll(v, 1, 0))
        beyond = jnp.where(line_no == lines - 1, under, pltpu.roll(v, lines - 1, 0))
        return average(v, before, beyond, node_y)

    for stage in range(3):
        def prepare(j, edges, stage=stage):
            west_edge, east_edge = edges
            for i in range(group):
                l = j * group + i
                if stage == 0:
                    value = heat_ref[at(l), :] - raw[at(l), :]
                else:
                    value = heat_ref[at(l), :] - wind(cur[at(l), :], l)
                raw[at(l), :] = value
                here = lane == l
                west_edge = jnp.where(here, pltpu.roll(value, l, 1), west_edge)
                east_edge = jnp.where(here, pltpu.roll(value, l + 1, 1), east_edge)
            return west_edge, east_edge

        nothing = jnp.zeros((lines, span), f32)
        west_edge, east_edge = lax.fori_loop(0, levels // group, prepare, (nothing, nothing))
        edgesnd[stage, 0] = west_edge
        edgesnd[stage, 1] = east_edge
        rowsnd[stage, 0] = raw[pl.ds(0, levels, stride=lines), :]
        rowsnd[stage, 1] = raw[pl.ds(lines - 1, levels, stride=lines), :]
        copies = []
        for n, device in enumerate(targets):
            if n < 6:
                source, sink = edgesnd.at[stage, 1 - n // 3], edgegot.at[stage, n]
            else:
                source, sink = rowsnd.at[stage, 7 - n], rowgot.at[stage, n - 6]
            copies.append(
                pltpu.make_async_remote_copy(
                    src_ref=source, dst_ref=sink, send_sem=halo_send.at[stage, n],
                    recv_sem=halo_recv.at[stage, n], device_id=device, device_id_type=MESH,
                )
            )
        for copy in copies:
            copy.start()
        for copy in copies:
            copy.wait_recv()
        beside = [
            average_y(
                edgegot[stage, 3 * side],
                edgegot[stage, 3 * side + 1, lines - 1 : lines, :],
                edgegot[stage, 3 * side + 2, 0:1, :],
            )
            for side in range(2)
        ]

        def finish(j, carry, stage=stage, beside=beside):
            for i in range(group):
                l = j * group + i
                value = average_y(
                    raw[at(l), :], rowgot[stage, 0, pl.ds(l, 1), :], rowgot[stage, 1, pl.ds(l, 1), :]
                )
                before = jnp.where(
                    lane == 0, pltpu.roll(beside[0], span - l, 1), pltpu.roll(value, 1, 1)
                )
                beyond = jnp.where(
                    lane == span - 1,
                    pltpu.roll(beside[1], span - 1 - l, 1),
                    pltpu.roll(value, span - 1, 1),
                )
                step = TIME_INCREMENT * average(value, before, beyond, node_x)
                start = temp_ref[at(l), :]
                if stage == 0:
                    cur[at(l), :] = start + step
                elif stage == 1:
                    cur[at(l), :] = 0.75 * start + 0.25 * (cur[at(l), :] + step)
                else:
                    adv_ref[at(l), :] = 1.0 / 3.0 * start + 2.0 / 3.0 * (cur[at(l), :] + step)
            return carry

        lax.fori_loop(0, levels // group, finish, 0)
        for copy in copies:
            copy.wait_send()
    for h in range(2):
        state_copy(h).wait_send()
        heat_copy(h).wait_send()


def solution(mesh):
    nx, ny = mesh.shape["gx"], mesh.shape["gy"]

    def local(
        atmospheric_constituents,
        thermal_ratio,
        flow_velocity,
        solar_elevation_factor,
        ground_reflectivity,
        sunlit_indicator,
        molecular_optics_lookup,
        condensate_optics_lookup,
    ):
        f32 = jnp.float32
        levels, lines, span = thermal_ratio.shape
        gtot = condensate_optics_lookup.shape[1]
        total = levels * lines
        wide = lines // 4 * span
        rows = FIELDS * levels + 8
        dma = pltpu.SemaphoreType.DMA
        heat, advected = pl.pallas_call(
            functools.partial(whole_kernel, nx, ny),
            out_shape=[jax.ShapeDtypeStruct((total, span), f32)] * 2,
            in_specs=[pl.BlockSpec(memory_space=pltpu.VMEM)] * 8,
            out_specs=[pl.BlockSpec(memory_space=pltpu.VMEM)] * 2,
            scratch_shapes=[
                pltpu.VMEM((2, rows, wide), f32),
                pltpu.VMEM((2, rows, wide), f32),
                pltpu.VMEM((2, wide // span, 8 * levels, span), f32),
                pltpu.VMEM((2, 3 * gtot, wide), f32),
                pltpu.VMEM((gtot, wide), f32),
                pltpu.VMEM((gtot, wide), f32),
                pltpu.VMEM((levels + 1, gtot, wide), f32),
                pltpu.VMEM((levels, gtot, wide), f32),
                pltpu.VMEM((levels, gtot, wide), f32),
                pltpu.VMEM((levels + 8, wide), f32),
                pltpu.VMEM((2, levels, wide), f32),
                pltpu.VMEM((2, levels, wide), f32),
                pltpu.VMEM((total, span), f32),
                pltpu.VMEM((total, span), f32),
                pltpu.VMEM((3, 2, levels, span), f32),
                pltpu.VMEM((3, 2, levels, span), f32),
                pltpu.VMEM((3, 2, lines, span), f32),
                pltpu.VMEM((3, 6, lines, span), f32),
                dma((2,)), dma((2,)), dma((2,)), dma((2,)), dma((3, 8)), dma((3, 8)),
            ],
            compiler_params=pltpu.CompilerParams(
                vmem_limit_bytes=58 * 2**20, collective_id=0, has_side_effects=True
            ),
            name="shortwave_advection",
        )(
            atmospheric_constituents.reshape(FIELDS * total, span),
            thermal_ratio.reshape(total, span),
            flow_velocity.reshape(2 * total, span),
            solar_elevation_factor,
            ground_reflectivity,
            sunlit_indicator,
            coef_matrix(molecular_optics_lookup, condensate_optics_lookup),
            condensate_optics_lookup[6][:, None],
        )
        return (heat.reshape(levels, lines, span), advected.reshape(levels, lines, span))

    in_specs = (
        P(None, None, "gy", "gx"),
        P(None, "gy", "gx"),
        P(None, None, "gy", "gx"),
        P("gy", "gx"),
        P("gy", "gx"),
        P("gy", "gx"),
        P(),
        P(),
    )
    out_specs = (P(None, "gy", "gx"), P(None, "gy", "gx"))
    return jax.shard_map(local, mesh=mesh, in_specs=in_specs, out_specs=out_specs, check_vma=False)
```

time: 147 us -> 102 us (0.69)
  waiting for transfers between devices: 42.6 us -> 0 us
  Pallas kernels: 46.7 us -> 88.5 us
  starting transfers between devices: 26.7 us -> 0 us
  local copies, waits for them, and re-layouts: 18.2 us -> 9.38 us
  other arithmetic: 6.83 us -> 2.78 us
  matrix products: 3.34 us -> 0 us
    ppermute x15 -> x0, waiting for transfers between devices: 42.6 us -> none  [the longest x6 20.9 us: padded_2(): lax.ppermute(lax.slice_in_dim(block, 0, width, axis=dim), axis, backward)]
    pallas_call x2 -> x1, Pallas kernels: 46.7 us -> 88.5 us  [local(): pl.pallas_call(functools.partial(whole_kernel, nx, ny), out_shape=[jax.Sh...]
    ppermute x15 -> x0, starting transfers between devices: 26.7 us -> none  [the longest x6 10.3 us: padded_2(): lax.ppermute(lax.slice_in_dim(block, 0, width, axis=dim), axis, backward)]
    concatenate x3 -> x1, local copies, waits for them, and re-layouts: 5.52 us -> 0.08 us  [coef_matrix(): wide = jnp.concatenate([high, high, low, jnp.zeros_like(high)], axis=-1)]
    select_n x9 -> x0, other arithmetic: 4.38 us -> none  [the longest x2 1.54 us: theirs(): return jnp.where(low, value[..., half:, :], value[..., :half, :])]
    dot_general x6 -> x0, matrix products: 3.34 us -> none  [the longest x3 1.88 us: warming_change_rate(): jnp.einsum('ij,ljx->lix', y_derivative, field_now, precision=lax.Precisio...]
    slice x10 -> x0, local copies, waits for them, and re-layouts: 2.73 us -> none  [the longest x1 1.28 us: local(): atmospheric_constituents[0]]
    convert_element_type x0 -> x1, local copies, waits for them, and re-layouts: none -> 2.2 us  [coef_matrix(): wide.reshape(levels // PACK, 3 * gpoints, PACK * 32).astype(jnp.bfloat16)]
  transfers between devices with their start and end apart: 15 -> 0, of which waited for: 12 -> 0; matrix products, arithmetic and copies ran while one was open for 9% -> 0% of each run, Pallas kernels for 0% -> 0%
where the time goes in v2:
time: 102 us; the launch traced here: 101 us
  Pallas kernels  88.5 us (87%)
  local copies, waits for them, and re-layouts  9.38 us (9%)
  other arithmetic  2.78 us (3%)
    pallas_call x1, Pallas kernels, local(): pl.pallas_call(functools.partial(whole_kernel, nx, ny), out_shape=[jax.Sh...  88.5 us
    unnamed x2, local copies, waits for them, and re-layouts  3.39 us
    convert_element_type x1, local copies, waits for them, and re-layouts, coef_matrix(): wide.reshape(levels // PACK, 3 * gpoints, PACK * 32).astype(jnp.bfloat16)  2.2 us

profile of v2, /device:TPU:1, one launch (start us, length us, event | category | flops | bytes accessed | tf_op | source)
XLA Modules:
  0.0 101.4 jit_solution(3177675755302925477)
XLA Ops:
  0.6 0.9 bitcast_multiply_fusion.7
  1.6 0.8 bitcast_multiply_fusion
  2.5 0.4 stack.56
  3.0 0.8 fusion.3
  3.8 0.4 stack.61
  4.3 0.4 stack.65
  4.7 0.4 reduce-precision_convert_fusion
  5.1 0.1 pad.3.clone
  5.2 0.7 maximum_maximum_fusion
  5.9 2.2 %copy.23.lhs_ref = bf16[18,336,128]{2,1,0:T(8,128)(2,1)} copy(bf16[18,336,128]{1,2,0:T(8,128)(2,1)S(1)} %bitcast.69) | data formatting | bytes 3096576 | tf_op jit(solution)/shard_map/convert_element_type | solution.py:52
  8.1 0.7 slice_bitcast_fusion
  8.8 0.7 copy.24.w_ref
  9.5 88.5 %shortwave_advection.1 = (f32[576,128]{1,0:T(8,128)}, f32[576,128]{1,0:T(8,128)}) custom-call(f32[2880,128]{1,0:T(8,128)} %bitcast.70, f32[576,128]{1,0:T(8,128)} %bitcast.72, f32[1152,128]{1,0:T(8,128)} %bitcast.71, f32[8,128]{1,0:T(8,128)} %mu_ref.1, f32[8,128]{1,0:T(8,128)} %ground_ref.1, s32[8,128]{1,0:T(8,128)} %day_ref.1, ...), custom_call_target="tpu_custom_call" | custom-call | tf_op jit(solution)/shard_map/shortwave_advection/pallas_call | solution.py:422
  98.0 1.7 %copy.27 = f32[72,8,128]{2,1,0:T(8,128)} copy(f32[72,8,128]{2,1,0:T(8,128)} %bitcast.74) | data formatting | bytes 589824
  99.7 1.7 %copy.28 = f32[72,8,128]{2,1,0:T(8,128)} copy(f32[72,8,128]{2,1,0:T(8,128)} %bitcast.73) | data formatting | bytes 589824
  (9 shorter events, 0.2 us)

commit v3 on v2

--- a/solution.py
+++ b/solution.py
@@ -13,7 +13,7 @@
 LOG2E = 1.4426950408889634
 MESH = pl.DeviceIdType.MESH
 FIELDS = 5
-PACK = 4
+LANES = 8
 
 
 def gll_derivative():
@@ -31,50 +31,84 @@
     return derivative
 
 
-def coef_matrix(mol, tab):
-    k0, k1, k2 = mol[0].T, mol[1].T, mol[2].T
-    levels, gpoints = k0.shape
-    zero = jnp.zeros_like(k0)
-    lext, lalb, lasy, iext, ialb, iasy = (
-        jnp.broadcast_to(tab[i][None, :], k0.shape) for i in range(6)
-    )
-    pad = [zero] * 3
-    depth = jnp.stack([2 * k0, 2 * k1, 2 * k2, 2 * lext, 2 * iext] + pad, -1)
-    absorb = jnp.stack([k0, k1, zero, lext * (1 - lalb), iext * (1 - ialb)] + pad, -1)
-    back = jnp.stack(
-        [zero, zero, k2, lext * lalb * (1 - lasy), iext * ialb * (1 - iasy)] + pad, -1
-    )
-    coefs = jnp.concatenate([depth, absorb, back], axis=1)
-    high = lax.reduce_precision(coefs, 8, 7)
-    low = coefs - high
-    wide = jnp.concatenate([high, high, low, jnp.zeros_like(high)], axis=-1)
-    wide = wide.reshape(levels // PACK, PACK, 3 * gpoints, 32).transpose(0, 2, 1, 3)
-    return wide.reshape(levels // PACK, 3 * gpoints, PACK * 32).astype(jnp.bfloat16)
-
-
-def shortwave(x_ref, mu, ground, lhs_ref, w_ref, out_ref, mm, beam, src, a_all, p_all, o_all, flux):
+def build_coefs(mol_ref, tab_ref, lhs_ref, w_ref, mols, waters):
+    f32 = jnp.float32
+    gtot, span = w_ref.shape[0], mols.shape[1]
+    levels = mol_ref.shape[2]
+    mols[...] = jnp.zeros_like(mols)
+    for k in range(3):
+        mols[k * gtot : (k + 1) * gtot, 0:levels] = mol_ref[k]
+    waters[...] = jnp.zeros_like(waters)
+    waters[0 : tab_ref.shape[0], 0:gtot] = tab_ref[...]
+    table = waters[...].T
+    w_ref[...] = table[0:gtot, 6:7]
+    tile = 16
+    lane = lax.broadcasted_iota(jnp.int32, (tile, span), 1)
+    field = lane // LANES
+
+    for i in range(gtot // tile):
+        rows = slice(i * tile, (i + 1) * tile)
+        lext, lalb, lasy, iext, ialb, iasy = (
+            jnp.broadcast_to(table[rows, k : k + 1], (tile, span)) for k in range(6)
+        )
+
+        def water(liquid, ice):
+            return jnp.where(field == 3, liquid, jnp.where(field == 4, ice, 0.0))
+
+        fixed = [
+            water(lext, iext),
+            water(lext * (1 - lalb), iext * (1 - ialb)),
+            water(lext * lalb * (1 - lasy), iext * ialb * (1 - iasy)),
+        ]
+
+        @pl.loop(0, lhs_ref.shape[0])
+        def _(c, i=i, fixed=fixed):
+            k0, k1, k2 = (
+                pltpu.roll(
+                    mols[pl.ds(k * gtot + i * tile, tile), :],
+                    lax.rem(span + LANES * k - LANES * c, span),
+                    1,
+                )
+                for k in range(3)
+            )
+            gas = jnp.where(field == 0, k0, jnp.where(field == 1, k1, 0.0))
+            rayleigh = jnp.where(field == 2, k2, 0.0)
+            sums = [2.0 * (fixed[0] + gas + rayleigh), fixed[1] + gas, fixed[2] + rayleigh]
+            for n, value in enumerate(sums):
+                high = value.astype(jnp.bfloat16).astype(f32)
+                low = value - high
+                wide = (
+                    high
+                    + pltpu.roll(high, FIELDS * LANES, 1)
+                    + pltpu.roll(low, 2 * FIELDS * LANES, 1)
+                )
+                lhs_ref[c, pl.ds(n * gtot + i * tile, tile), :] = wide.astype(jnp.bfloat16)
+
+
+def shortwave(
+    prepare, base_ref, mask_ref, mu, ground, lhs_ref, w_ref, out_ref,
+    mm, beam, src, a_all, p_all, o_all, flux,
+):
     levels, gtot, n = p_all.shape
     blocks = gtot // 8
+    chunks = levels // LANES
     f32 = jnp.float32
     nc = jnp.broadcast_to((-0.5 * LOG2E) / mu, (8, n))
 
-    def mults(l, slot):
-        x = jnp.concatenate(
-            [x_ref[r, pl.ds(l, 8, stride=levels), :] for r in range(x_ref.shape[0])], axis=1
-        )
-        high = x.astype(jnp.bfloat16).astype(f32)
-        low = x - high
-        nil = jnp.zeros_like(high)
-        inner = lax.rem(l, PACK)
-        parts = []
-        for j in range(PACK):
-            hit = inner == j
-            h = jnp.where(hit, high, nil)
-            parts += [h, jnp.where(hit, low, nil), h, nil]
-        rhs = jnp.concatenate(parts, axis=0).astype(jnp.bfloat16)
-        mm[slot] = jnp.dot(lhs_ref[l // PACK], rhs, preferred_element_type=f32)
-
-    mults(0, 0)
+    pieces = 3
+
+    def right_side(l):
+        return base_ref[lax.rem(l // LANES, 2)] * mask_ref[lax.rem(l, LANES)]
+
+    def multiply(l, slot, rhs, piece):
+        rows = pl.ds(gtot * piece, gtot)
+        mm[slot, rows, :] = jnp.dot(
+            lhs_ref[l // LANES, rows, :], rhs, preferred_element_type=f32
+        )
+
+    prepare(0)
+    for piece in range(pieces):
+        multiply(0, 0, right_side(0), piece)
     acc = jnp.zeros((8, n), f32)
     for i in range(blocks):
         sl = pl.ds(8 * i, 8)
@@ -86,8 +120,12 @@
     flux[0:1, :] = jnp.sum(acc, axis=0, keepdims=True)
 
     def down(l, slot):
+        later = jnp.minimum(l + 1, levels - 1)
+        rhs = right_side(later)
         acc = jnp.zeros((8, n), f32)
         for i in range(blocks):
+            if i % 5 == 0:
+                multiply(later, 1 - slot, rhs, i // 5)
             sl = pl.ds(8 * i, 8)
             t2 = mm[slot, sl, :]
             a = mm[slot, pl.ds(gtot + 8 * i, 8), :]
@@ -99,11 +137,12 @@
             pr = a * c
             q = pr * lax.rsqrt(pr)
             t = jnp.tanh(q)
-            u = q * (t * t)
             x = a + c
-            rden = 1.0 / (t * x + (q + u))
-            refl = (t * b) * rden
-            tran = (q - u) * rden
+            outer = q * (1.0 / t)
+            inner = q * t
+            rden = 1.0 / (x + outer + inner)
+            refl = b * rden
+            tran = (outer - inner) * rden
             bn = bm * jnp.exp2(t2 * nc)
             lost = bm - bn
             w = lost * (1.0 / t2)
@@ -122,13 +161,17 @@
             acc = acc + (bn + s1)
         flux[pl.ds(l + 1, 1), :] = jnp.sum(acc, axis=0, keepdims=True)
 
-    @pl.loop(0, levels // 2)
-    def _(h):
-        l = 2 * h
-        mults(l + 1, 1)
-        down(l, 0)
-        mults(jnp.minimum(l + 2, levels - 1), 0)
-        down(l + 1, 1)
+    @pl.loop(0, chunks)
+    def _(c):
+        @pl.when(c + 1 < chunks)
+        def _():
+            prepare(c + 1)
+
+        @pl.loop(0, LANES // 2)
+        def _(h):
+            l = c * LANES + 2 * h
+            down(l, 0)
+            down(l + 1, 1)
 
     ups = []
     acc = jnp.zeros((8, n), f32)
@@ -159,11 +202,11 @@
 
 
 def whole_kernel(
-    nx, ny, state_ref, temp_ref, flow_ref, mu_ref, ground_ref, day_ref, lhs_ref, w_ref,
+    nx, ny, state_ref, temp_ref, flow_ref, mu_ref, ground_ref, day_ref, mol_ref, tab_ref,
     heat_ref, adv_ref,
-    snd, got, xs, mm, beam, src, a_all, p_all, o_all, flux, hwork, hgot,
+    snd, got, sfcsnd, sfcgot, base, mask, lhs_ref, w_ref, mols, waters, mm, beam, src, a_all, p_all, o_all, flux, hwork, hgot,
     raw, cur, rowsnd, rowgot, edgesnd, edgegot,
-    state_send, state_recv, heat_send, heat_recv, halo_send, halo_recv,
+    state_send, state_recv, sfc_send, sfc_recv, heat_send, heat_recv, halo_send, halo_recv,
 ):
     f32 = jnp.float32
     gx, gy = lax.axis_index("gx"), lax.axis_index("gy")
@@ -188,26 +231,33 @@
         pl.semaphore_signal(barrier, inc=1, device_id=device, device_id_type=MESH)
     pl.semaphore_wait(barrier, len(targets) + 1)
 
-    def products(line, store):
-        line_of = lambda ref, k: ref[pl.ds(k * total + line, levels, stride=lines), :]
+    chunks = levels // LANES
+
+    def products(line, c):
+        def line_of(ref, k):
+            return ref[pl.ds(k * total + c * (LANES * lines) + line, LANES, stride=lines), :]
+
         temper = line_of(temp_ref, 0)
         thick = line_of(state_ref, 2)
         weighted = thick * temper * temper
-        values = [
+        return [
             weighted * line_of(state_ref, 0),
             weighted * line_of(state_ref, 1),
             thick,
             line_of(state_ref, 3),
             line_of(state_ref, 4),
         ]
-        for k, value in enumerate(values):
-            store(slice(k * levels, (k + 1) * levels), value)
-
-    def state_copy(h):
+
+    def state_copy(h, c):
         return pltpu.make_async_remote_copy(
-            src_ref=snd.at[h], dst_ref=got.at[h], send_sem=state_send.at[h],
-            recv_sem=state_recv.at[h], device_id=(far, gy), device_id_type=MESH,
-        )
+            src_ref=snd.at[h, c], dst_ref=got.at[h, c], send_sem=state_send.at[h, c],
+            recv_sem=state_recv.at[h, c], device_id=(far, gy), device_id_type=MESH,
+        )
+
+    surface_copy = pltpu.make_async_remote_copy(
+        src_ref=sfcsnd, dst_ref=sfcgot, send_sem=sfc_send, recv_sem=sfc_recv,
+        device_id=(far, gy), device_id_type=MESH,
+    )
 
     def heat_copy(h):
         return pltpu.make_async_remote_copy(
@@ -215,29 +265,26 @@
             recv_sem=heat_recv.at[h], device_id=(far, gy), device_id_type=MESH,
         )
 
-    tail = FIELDS * levels
-    for h in range(2):
+    for n in range(half):
+        line = pl.ds(theirs + n, 1)
+        sfcsnd[n : n + 1, :] = mu_ref[line, :]
+        sfcsnd[half + n : half + n + 1, :] = ground_ref[line, :]
+    surface_copy.start()
+
+    def send_state(h, c):
         for r in range(pair):
-            lanes = slice(r * span, (r + 1) * span)
-            line = theirs + pair * h + r
-
-            def to_send(rows, value, h=h, lanes=lanes):
-                snd[h, rows, lanes] = value
-
-            products(line, to_send)
-            snd[h, tail : tail + 1, lanes] = mu_ref[pl.ds(line, 1), :]
-            snd[h, tail + 1 : tail + 2, lanes] = ground_ref[pl.ds(line, 1), :]
-            snd[h, tail + 2 : tail + 8, lanes] = jnp.zeros((6, span), f32)
-        state_copy(h).start()
-
-    for h in range(2):
-        for r in range(pair):
-            xs[h, r, tail:, :] = jnp.zeros((xs.shape[2] - tail, span), f32)
-
-            def to_own(rows, value, h=h, r=r):
-                xs[h, r, rows, :] = value
-
-            products(mine + pair * h + r, to_own)
+            for k, value in enumerate(products(theirs + pair * h + r, c)):
+                snd[h, c, k * LANES : (k + 1) * LANES, r * span : (r + 1) * span] = value
+        state_copy(h, c).start()
+
+    @pl.loop(0, chunks)
+    def _(c):
+        send_state(0, c)
+
+    build_coefs(mol_ref, tab_ref, lhs_ref, w_ref, mols, waters)
+    row_no = lax.broadcasted_iota(jnp.int32, mask.shape[1:], 0)
+    for j in range(LANES):
+        mask[j] = jnp.where(lax.rem(row_no, LANES) == j, 1.0, 0.0).astype(jnp.bfloat16)
 
     dref = gll_derivative()
     lane = lax.broadcasted_iota(jnp.int32, (lines, span), 1)
@@ -279,20 +326,39 @@
             l = j * group + i
             raw[at(l), :] = wind(temp_ref[at(l), :], l)
 
+    surface_copy.wait_recv()
     for h in range(2):
-        state_copy(h).wait_recv()
         mus, grounds = [], []
         for r in range(pair):
-            lanes = slice(r * span, (r + 1) * span)
             line = pl.ds(mine + pair * h + r, 1)
             own = day_ref[line, :] == 1
-            for k in range(FIELDS):
-                rows = slice(k * levels, (k + 1) * levels)
-                xs[h, r, rows, :] = jnp.where(own, xs[h, r, rows, :], got[h, rows, lanes])
-            mus.append(jnp.where(own, mu_ref[line, :], got[h, tail : tail + 1, lanes]))
-            grounds.append(jnp.where(own, ground_ref[line, :], got[h, tail + 1 : tail + 2, lanes]))
+            n = pair * h + r
+            mus.append(jnp.where(own, mu_ref[line, :], sfcgot[n : n + 1, :]))
+            grounds.append(
+                jnp.where(own, ground_ref[line, :], sfcgot[half + n : half + n + 1, :])
+            )
+
+        def prepare(c, h=h):
+            state_copy(h, c).wait_recv()
+            if h == 0:
+                send_state(1, c)
+            highs, lows = [[] for _ in range(FIELDS)], [[] for _ in range(FIELDS)]
+            for r in range(pair):
+                line = mine + pair * h + r
+                own = day_ref[pl.ds(line, 1), :] == 1
+                for k, value in enumerate(products(line, c)):
+                    other = got[h, c, k * LANES : (k + 1) * LANES, r * span : (r + 1) * span]
+                    value = jnp.where(own, value, other)
+                    high = value.astype(jnp.bfloat16).astype(f32)
+                    highs[k].append(high)
+                    lows[k].append(value - high)
+            highs = [jnp.concatenate(v, axis=1) for v in highs]
+            lows = [jnp.concatenate(v, axis=1) for v in lows]
+            parts = highs + lows + highs + [jnp.zeros_like(highs[0])]
+            base[lax.rem(c, 2)] = jnp.concatenate(parts, axis=0).astype(jnp.bfloat16)
+
         shortwave(
-            xs.at[h], jnp.concatenate(mus, axis=1), jnp.concatenate(grounds, axis=1),
+            prepare, base, mask, jnp.concatenate(mus, axis=1), jnp.concatenate(grounds, axis=1),
             lhs_ref, w_ref, hwork.at[h], mm, beam, src, a_all, p_all, o_all, flux,
         )
         heat_copy(h).start()
@@ -394,9 +460,18 @@
         lax.fori_loop(0, levels // group, finish, 0)
         for copy in copies:
             copy.wait_send()
+    surface_copy.wait_send()
     for h in range(2):
-        state_copy(h).wait_send()
         heat_copy(h).wait_send()
+
+        @pl.loop(0, chunks)
+        def _(c, h=h):
+            state_copy(h, c).wait_send()
+
+
+def finish_kernel(heat_ref, adv_ref, heat_out, adv_out):
+    heat_out[...] = heat_ref[...]
+    adv_out[...] = adv_ref[...]
 
 
 def solution(mesh):
@@ -417,7 +492,7 @@
         gtot = condensate_optics_lookup.shape[1]
         total = levels * lines
         wide = lines // 4 * span
-        rows = FIELDS * levels + 8
+        chunks = levels // LANES
         dma = pltpu.SemaphoreType.DMA
         heat, advected = pl.pallas_call(
             functools.partial(whole_kernel, nx, ny),
@@ -425,9 +500,16 @@
             in_specs=[pl.BlockSpec(memory_space=pltpu.VMEM)] * 8,
             out_specs=[pl.BlockSpec(memory_space=pltpu.VMEM)] * 2,
             scratch_shapes=[
-                pltpu.VMEM((2, rows, wide), f32),
-                pltpu.VMEM((2, rows, wide), f32),
-                pltpu.VMEM((2, wide // span, 8 * levels, span), f32),
+                pltpu.VMEM((2, chunks, FIELDS * LANES, wide), f32),
+                pltpu.VMEM((2, chunks, FIELDS * LANES, wide), f32),
+                pltpu.VMEM((lines, span), f32),
+                pltpu.VMEM((lines, span), f32),
+                pltpu.VMEM((2, 128, wide), jnp.bfloat16),
+                pltpu.VMEM((LANES, 128, wide), jnp.bfloat16),
+                pltpu.VMEM((chunks, 3 * gtot, 128), jnp.bfloat16),
+                pltpu.VMEM((gtot, 1), f32),
+                pltpu.VMEM((3 * gtot, 128), f32),
+                pltpu.VMEM((8, 128), f32),
                 pltpu.VMEM((2, 3 * gtot, wide), f32),
                 pltpu.VMEM((gtot, wide), f32),
                 pltpu.VMEM((gtot, wide), f32),
@@ -443,7 +525,8 @@
                 pltpu.VMEM((3, 2, levels, span), f32),
                 pltpu.VMEM((3, 2, lines, span), f32),
                 pltpu.VMEM((3, 6, lines, span), f32),
-                dma((2,)), dma((2,)), dma((2,)), dma((2,)), dma((3, 8)), dma((3, 8)),
+                dma((2, chunks)), dma((2, chunks)), dma(()), dma(()), dma((2,)), dma((2,)),
+                dma((3, 8)), dma((3, 8)),
             ],
             compiler_params=pltpu.CompilerParams(
                 vmem_limit_bytes=58 * 2**20, collective_id=0, has_side_effects=True
@@ -456,9 +539,18 @@
             solar_elevation_factor,
             ground_reflectivity,
             sunlit_indicator,
-            coef_matrix(molecular_optics_lookup, condensate_optics_lookup),
-            condensate_optics_lookup[6][:, None],
-        )
+            molecular_optics_lookup,
+            condensate_optics_lookup,
+        )
+        spec = pl.BlockSpec((total // 3, span), lambda i: (i, 0))
+        heat, advected = pl.pallas_call(
+            finish_kernel,
+            grid=(3,),
+            out_shape=[jax.ShapeDtypeStruct((total, span), f32)] * 2,
+            in_specs=[spec] * 2,
+            out_specs=[spec] * 2,
+            name="results",
+        )(heat, advected)
         return (heat.reshape(levels, lines, span), advected.reshape(levels, lines, span))
 
     in_specs = (

time: 102 us -> 92.8 us (0.910)
  local copies, waits for them, and re-layouts: 9.38 us -> 1.69 us
  other arithmetic: 2.78 us -> 0 us
  Pallas kernels: 88.5 us -> 90.2 us
    another operation x13 -> x0, local copies, waits for them, and re-layouts: 2.89 us -> none  [the longest x2 1.42 us: local(): condensate_optics_lookup[6][:, None]]
    pallas_call x0 -> x1, Pallas kernels: none -> 2.76 us  [local(): pl.pallas_call(finish_kernel, grid=(3,), out_shape=[jax.ShapeDtypeStruct(...]
    convert_element_type x1 -> x0, local copies, waits for them, and re-layouts: 2.2 us -> none  [coef_matrix(): wide.reshape(levels // PACK, 3 * gpoints, PACK * 32).astype(jnp.bfloat16)]
    mul x2 -> x0, other arithmetic: 1.73 us -> none  [coef_matrix(): depth = jnp.stack([2 * k0, 2 * k1, 2 * k2, 2 * lext, 2 * iext] + pad, -1)]
    unnamed x2 -> x1, local copies, waits for them, and re-layouts: 3.39 us -> 1.69 us
    pallas_call x1, Pallas kernels: 88.5 us -> 87.4 us  [local(): pl.pallas_call(functools.partial(whole_kernel, nx, ny), out_shape=[jax.Sh...]
where the time goes in v3:
time: 92.8 us; the launch traced here: 92.5 us
  Pallas kernels  90.2 us (97%)
  local copies, waits for them, and re-layouts  1.69 us (2%)
    pallas_call x1, Pallas kernels, local(): pl.pallas_call(functools.partial(whole_kernel, nx, ny), out_shape=[jax.Sh...  87.4 us
    pallas_call x1, Pallas kernels, local(): pl.pallas_call(finish_kernel, grid=(3,), out_shape=[jax.ShapeDtypeStruct(...  2.76 us

profile of v3, /device:TPU:1, one launch (start us, length us, event | category | flops | bytes accessed | tf_op | source)
XLA Modules:
  0.0 92.5 jit_solution(935514104809718265)
XLA Ops:
  0.6 1.7 %copy.10.mol_ref = f32[3,112,72]{2,1,0:T(8,128)} copy(f32[3,112,72]{1,2,0:T(8,128)} %param.14) | data formatting | bytes 193536 | tf_op args[6]
  2.3 87.4 %shortwave_advection.1 = (f32[576,128]{1,0:T(8,128)}, f32[576,128]{1,0:T(8,128)}) custom-call(f32[2880,128]{1,0:T(8,128)} %bitcast.5, f32[576,128]{1,0:T(8,128)} %bitcast.7, f32[1152,128]{1,0:T(8,128)} %bitcast.6, f32[8,128]{1,0:T(8,128)} %mu_ref.1, f32[8,128]{1,0:T(8,128)} %ground_ref.1, s32[8,128]{1,0:T(8,128)} %day_ref.1, f32[3,112,72]{2,1,0:T(8,128)} %copy.10.mol_ref, ...), custom_call_target="tpu_custom_call" | custom-call | tf_op jit(solution)/shard_map/shortwave_advection/pallas_call | solution.py:497
  89.7 2.8 %results.1 = (f32[576,128]{1,0:T(8,128)}, f32[576,128]{1,0:T(8,128)}) custom-call(f32[576,128]{1,0:T(8,128)} %get-tuple-element.6.heat_ref, f32[576,128]{1,0:T(8,128)} %get-tuple-element.7.adv_ref), custom_call_target="tpu_custom_call" | custom-call | tf_op jit(solution)/shard_map/results/pallas_call | solution.py:546

commit v4 on v3

--- a/solution.py
+++ b/solution.py
@@ -14,6 +14,7 @@
 MESH = pl.DeviceIdType.MESH
 FIELDS = 5
 LANES = 8
+PARTS = 3
 
 
 def gll_derivative():
@@ -31,13 +32,14 @@
     return derivative
 
 
-def build_coefs(mol_ref, tab_ref, lhs_ref, w_ref, mols, waters):
+def build_coefs(mol_ref, tab_ref, lhs_ref, w_ref, mols, waters, flip):
     f32 = jnp.float32
     gtot, span = w_ref.shape[0], mols.shape[1]
-    levels = mol_ref.shape[2]
-    mols[...] = jnp.zeros_like(mols)
+    levels = mol_ref.shape[1]
     for k in range(3):
-        mols[k * gtot : (k + 1) * gtot, 0:levels] = mol_ref[k]
+        flip[...] = jnp.zeros_like(flip)
+        flip[0:levels, 0:gtot] = mol_ref[k]
+        mols[k * gtot : (k + 1) * gtot, :] = flip[...].T[0:gtot, :]
     waters[...] = jnp.zeros_like(waters)
     waters[0 : tab_ref.shape[0], 0:gtot] = tab_ref[...]
     table = waters[...].T
@@ -204,7 +206,7 @@
 def whole_kernel(
     nx, ny, state_ref, temp_ref, flow_ref, mu_ref, ground_ref, day_ref, mol_ref, tab_ref,
     heat_ref, adv_ref,
-    snd, got, sfcsnd, sfcgot, base, mask, lhs_ref, w_ref, mols, waters, mm, beam, src, a_all, p_all, o_all, flux, hwork, hgot,
+    snd, got, sfcsnd, sfcgot, base, mask, lhs_ref, w_ref, mols, waters, flip, mm, beam, src, a_all, p_all, o_all, flux, hwork, hgot,
     raw, cur, rowsnd, rowgot, edgesnd, edgegot,
     state_send, state_recv, sfc_send, sfc_recv, heat_send, heat_recv, halo_send, halo_recv,
 ):
@@ -281,7 +283,7 @@
     def _(c):
         send_state(0, c)
 
-    build_coefs(mol_ref, tab_ref, lhs_ref, w_ref, mols, waters)
+    build_coefs(mol_ref, tab_ref, lhs_ref, w_ref, mols, waters, flip)
     row_no = lax.broadcasted_iota(jnp.int32, mask.shape[1:], 0)
     for j in range(LANES):
         mask[j] = jnp.where(lax.rem(row_no, LANES) == j, 1.0, 0.0).astype(jnp.bfloat16)
@@ -387,11 +389,30 @@
         beyond = jnp.where(line_no == lines - 1, under, pltpu.roll(v, lines - 1, 0))
         return average(v, before, beyond, node_y)
 
-    for stage in range(3):
-        def prepare(j, edges, stage=stage):
+    parts = rowsnd.shape[1]
+    depth = levels // parts
+    steps = depth // group
+
+    def halo_copies(stage, g):
+        copies = []
+        for n, device in enumerate(targets):
+            if n < 6:
+                source, sink = edgesnd.at[stage, g, 1 - n // 3], edgegot.at[stage, g, n]
+            else:
+                source, sink = rowsnd.at[stage, g, 7 - n], rowgot.at[stage, g, n - 6]
+            copies.append(
+                pltpu.make_async_remote_copy(
+                    src_ref=source, dst_ref=sink, send_sem=halo_send.at[stage, g, n],
+                    recv_sem=halo_recv.at[stage, g, n], device_id=device, device_id_type=MESH,
+                )
+            )
+        return copies
+
+    def emit(stage, g):
+        def prepare(j, edges):
             west_edge, east_edge = edges
             for i in range(group):
-                l = j * group + i
+                l = g * depth + j * group + i
                 if stage == 0:
                     value = heat_ref[at(l), :] - raw[at(l), :]
                 else:
@@ -403,41 +424,34 @@
             return west_edge, east_edge
 
         nothing = jnp.zeros((lines, span), f32)
-        west_edge, east_edge = lax.fori_loop(0, levels // group, prepare, (nothing, nothing))
-        edgesnd[stage, 0] = west_edge
-        edgesnd[stage, 1] = east_edge
-        rowsnd[stage, 0] = raw[pl.ds(0, levels, stride=lines), :]
-        rowsnd[stage, 1] = raw[pl.ds(lines - 1, levels, stride=lines), :]
-        copies = []
-        for n, device in enumerate(targets):
-            if n < 6:
-                source, sink = edgesnd.at[stage, 1 - n // 3], edgegot.at[stage, n]
-            else:
-                source, sink = rowsnd.at[stage, 7 - n], rowgot.at[stage, n - 6]
-            copies.append(
-                pltpu.make_async_remote_copy(
-                    src_ref=source, dst_ref=sink, send_sem=halo_send.at[stage, n],
-                    recv_sem=halo_recv.at[stage, n], device_id=device, device_id_type=MESH,
-                )
-            )
-        for copy in copies:
+        west_edge, east_edge = lax.fori_loop(0, steps, prepare, (nothing, nothing))
+        edgesnd[stage, g, 0] = west_edge
+        edgesnd[stage, g, 1] = east_edge
+        for side, line in enumerate((0, lines - 1)):
+            rowsnd[stage, g, side] = raw[pl.ds(g * depth * lines + line, depth, stride=lines), :]
+        for copy in halo_copies(stage, g):
             copy.start()
-        for copy in copies:
+
+    def absorb(stage, g):
+        for copy in halo_copies(stage, g):
             copy.wait_recv()
         beside = [
             average_y(
-                edgegot[stage, 3 * side],
-                edgegot[stage, 3 * side + 1, lines - 1 : lines, :],
-                edgegot[stage, 3 * side + 2, 0:1, :],
+                edgegot[stage, g, 3 * side],
+                edgegot[stage, g, 3 * side + 1, lines - 1 : lines, :],
+                edgegot[stage, g, 3 * side + 2, 0:1, :],
             )
             for side in range(2)
         ]
 
-        def finish(j, carry, stage=stage, beside=beside):
+        def finish(j, carry):
             for i in range(group):
-                l = j * group + i
+                k = j * group + i
+                l = g * depth + k
                 value = average_y(
-                    raw[at(l), :], rowgot[stage, 0, pl.ds(l, 1), :], rowgot[stage, 1, pl.ds(l, 1), :]
+                    raw[at(l), :],
+                    rowgot[stage, g, 0, pl.ds(k, 1), :],
+                    rowgot[stage, g, 1, pl.ds(k, 1), :],
                 )
                 before = jnp.where(
                     lane == 0, pltpu.roll(beside[0], span - l, 1), pltpu.roll(value, 1, 1)
@@ -457,9 +471,19 @@
                     adv_ref[at(l), :] = 1.0 / 3.0 * start + 2.0 / 3.0 * (cur[at(l), :] + step)
             return carry
 
-        lax.fori_loop(0, levels // group, finish, 0)
-        for copy in copies:
-            copy.wait_send()
+        lax.fori_loop(0, steps, finish, 0)
+
+    for g in range(parts):
+        emit(0, g)
+    for stage in range(3):
+        for g in range(parts):
+            absorb(stage, g)
+            if stage < 2:
+                emit(stage + 1, g)
+    for stage in range(3):
+        for g in range(parts):
+            for copy in halo_copies(stage, g):
+                copy.wait_send()
     surface_copy.wait_send()
     for h in range(2):
         heat_copy(h).wait_send()
@@ -469,9 +493,26 @@
             state_copy(h, c).wait_send()
 
 
-def finish_kernel(heat_ref, adv_ref, heat_out, adv_out):
-    heat_out[...] = heat_ref[...]
-    adv_out[...] = adv_ref[...]
+def finish_kernel(heat_ref, adv_ref, heat_out, adv_out, hold, sems):
+    rows = hold.shape[2]
+    stages = []
+    for n, (source, sink) in enumerate(((heat_ref, heat_out), (adv_ref, adv_out))):
+        for part in range(hold.shape[1]):
+            here = pl.ds(part * rows, rows)
+            keep = hold.at[n, part]
+            stages.append(
+                (
+                    pltpu.make_async_copy(source.at[here], keep, sems.at[0, n, part]),
+                    pltpu.make_async_copy(keep, sink.at[here], sems.at[1, n, part]),
+                )
+            )
+    for first, _ in stages:
+        first.start()
+    for first, second in stages:
+        first.wait()
+        second.start()
+    for _, second in stages:
+        second.wait()
 
 
 def solution(mesh):
@@ -510,6 +551,7 @@
                 pltpu.VMEM((gtot, 1), f32),
                 pltpu.VMEM((3 * gtot, 128), f32),
                 pltpu.VMEM((8, 128), f32),
+                pltpu.VMEM((128, 128), f32),
                 pltpu.VMEM((2, 3 * gtot, wide), f32),
                 pltpu.VMEM((gtot, wide), f32),
                 pltpu.VMEM((gtot, wide), f32),
@@ -521,12 +563,12 @@
                 pltpu.VMEM((2, levels, wide), f32),
                 pltpu.VMEM((total, span), f32),
                 pltpu.VMEM((total, span), f32),
-                pltpu.VMEM((3, 2, levels, span), f32),
-                pltpu.VMEM((3, 2, levels, span), f32),
-                pltpu.VMEM((3, 2, lines, span), f32),
-                pltpu.VMEM((3, 6, lines, span), f32),
+                pltpu.VMEM((3, PARTS, 2, levels // PARTS, span), f32),
+                pltpu.VMEM((3, PARTS, 2, levels // PARTS, span), f32),
+                pltpu.VMEM((3, PARTS, 2, lines, span), f32),
+                pltpu.VMEM((3, PARTS, 6, lines, span), f32),
                 dma((2, chunks)), dma((2, chunks)), dma(()), dma(()), dma((2,)), dma((2,)),
-                dma((3, 8)), dma((3, 8)),
+                dma((3, PARTS, 8)), dma((3, PARTS, 8)),
             ],
             compiler_params=pltpu.CompilerParams(
                 vmem_limit_bytes=58 * 2**20, collective_id=0, has_side_effects=True
@@ -539,16 +581,15 @@
             solar_elevation_factor,
             ground_reflectivity,
             sunlit_indicator,
-            molecular_optics_lookup,
+            molecular_optics_lookup.transpose(0, 2, 1),
             condensate_optics_lookup,
         )
-        spec = pl.BlockSpec((total // 3, span), lambda i: (i, 0))
         heat, advected = pl.pallas_call(
             finish_kernel,
-            grid=(3,),
             out_shape=[jax.ShapeDtypeStruct((total, span), f32)] * 2,
-            in_specs=[spec] * 2,
-            out_specs=[spec] * 2,
+            in_specs=[pl.BlockSpec(memory_space=pl.ANY)] * 2,
+            out_specs=[pl.BlockSpec(memory_space=pl.ANY)] * 2,
+            scratch_shapes=[pltpu.VMEM((2, 2, total // 2, span), f32), dma((2, 2, 2))],
             name="results",
         )(heat, advected)
         return (heat.reshape(levels, lines, span), advected.reshape(levels, lines, span))

time: 92.8 us -> 88 us (0.948)
  Pallas kernels: 90.2 us -> 87.2 us
  local copies, waits for them, and re-layouts: 1.69 us -> 0 us
    pallas_call x1, Pallas kernels: 87.4 us -> 85.4 us  [local(): pl.pallas_call(functools.partial(whole_kernel, nx, ny), out_shape=[jax.Sh...]
    unnamed x1 -> x0, local copies, waits for them, and re-layouts: 1.69 us -> none
where the time goes in v4:
time: 88 us; the launch traced here: 87.9 us
  Pallas kernels  87.2 us (99%)
    pallas_call x1, Pallas kernels, local(): pl.pallas_call(functools.partial(whole_kernel, nx, ny), out_shape=[jax.Sh...  85.4 us
    pallas_call x1, Pallas kernels, local(): pl.pallas_call(finish_kernel, out_shape=[jax.ShapeDtypeStruct((total, spa...  1.85 us

profile of v4, /device:TPU:1, one launch (start us, length us, event | category | flops | bytes accessed | tf_op | source)
XLA Modules:
  0.0 87.9 jit_solution(13047862825404474755)
XLA Ops:
  0.6 85.4 %shortwave_advection.1 = (f32[576,128]{1,0:T(8,128)}, f32[576,128]{1,0:T(8,128)}) custom-call(f32[2880,128]{1,0:T(8,128)} %bitcast.6, f32[576,128]{1,0:T(8,128)} %bitcast.8, f32[1152,128]{1,0:T(8,128)} %bitcast.7, f32[8,128]{1,0:T(8,128)} %mu_ref.1, f32[8,128]{1,0:T(8,128)} %ground_ref.1, s32[8,128]{1,0:T(8,128)} %day_ref.1, f32[3,72,112]{2,1,0:T(8,128)} %bitcast.9, ...), custom_call_target="tpu_custom_call" | custom-call | tf_op jit(solution)/shard_map/shortwave_advection/pallas_call | solution.py:538
  86.0 1.9 %results.1 = (f32[576,128]{1,0:T(8,128)}, f32[576,128]{1,0:T(8,128)}) custom-call(f32[576,128]{1,0:T(8,128)} %get-tuple-element.6.heat_ref, f32[576,128]{1,0:T(8,128)} %get-tuple-element.7.adv_ref), custom_call_target="tpu_custom_call" | custom-call | tf_op jit(solution)/shard_map/results/pallas_call | solution.py:587

commit v5 on v4

--- a/solution.py
+++ b/solution.py
@@ -204,9 +204,9 @@
 
 
 def whole_kernel(
-    nx, ny, state_ref, temp_ref, flow_ref, mu_ref, ground_ref, day_ref, mol_ref, tab_ref,
+    nx, ny, state_hbm, temp_hbm, flow_hbm, mu_ref, ground_ref, day_ref, mol_ref, tab_ref,
     heat_ref, adv_ref,
-    snd, got, sfcsnd, sfcgot, base, mask, lhs_ref, w_ref, mols, waters, flip, mm, beam, src, a_all, p_all, o_all, flux, hwork, hgot,
+    state_ref, temp_ref, flow_ref, loads, snd, got, sfcsnd, sfcgot, base, mask, lhs_ref, w_ref, mols, waters, flip, mm, beam, src, a_all, p_all, o_all, flux, hwork, hgot,
     raw, cur, rowsnd, rowgot, edgesnd, edgegot,
     state_send, state_recv, sfc_send, sfc_recv, heat_send, heat_recv, halo_send, halo_recv,
 ):
@@ -228,6 +228,14 @@
         (west, gy), (west, south), (west, north),
         (gx, south), (gx, north),
     ]
+    inputs = [
+        pltpu.make_async_copy(source, sink, loads.at[n])
+        for n, (source, sink) in enumerate(
+            ((temp_hbm, temp_ref), (state_hbm, state_ref), (flow_hbm, flow_ref))
+        )
+    ]
+    for copy in inputs:
+        copy.start()
     barrier = pltpu.get_barrier_semaphore()
     for device in targets + [(far, gy)]:
         pl.semaphore_signal(barrier, inc=1, device_id=device, device_id_type=MESH)
@@ -267,6 +275,8 @@
             recv_sem=heat_recv.at[h], device_id=(far, gy), device_id_type=MESH,
         )
 
+    inputs[0].wait()
+    inputs[1].wait()
     for n in range(half):
         line = pl.ds(theirs + n, 1)
         sfcsnd[n : n + 1, :] = mu_ref[line, :]
@@ -321,6 +331,7 @@
         ] * slope(v, 0, lines, taps_y)
 
     group = 8
+    inputs[2].wait()
 
     @pl.loop(0, levels // group)
     def _(j):
@@ -538,9 +549,14 @@
         heat, advected = pl.pallas_call(
             functools.partial(whole_kernel, nx, ny),
             out_shape=[jax.ShapeDtypeStruct((total, span), f32)] * 2,
-            in_specs=[pl.BlockSpec(memory_space=pltpu.VMEM)] * 8,
+            in_specs=[pl.BlockSpec(memory_space=pl.ANY)] * 3
+            + [pl.BlockSpec(memory_space=pltpu.VMEM)] * 5,
             out_specs=[pl.BlockSpec(memory_space=pltpu.VMEM)] * 2,
             scratch_shapes=[
+                pltpu.VMEM((FIELDS * total, span), f32),
+                pltpu.VMEM((total, span), f32),
+                pltpu.VMEM((2 * total, span), f32),
+                dma((3,)),
                 pltpu.VMEM((2, chunks, FIELDS * LANES, wide), f32),
                 pltpu.VMEM((2, chunks, FIELDS * LANES, wide), f32),
                 pltpu.VMEM((lines, span), f32),

time: 88 us -> 87.3 us (level)
  no operation moved by 1% of the time
where the time goes in v5:
time: 87.3 us; the launch traced here: 87.2 us
  Pallas kernels  86.5 us (99%)
    pallas_call x1, Pallas kernels, local(): pl.pallas_call(functools.partial(whole_kernel, nx, ny), out_shape=[jax.Sh...  84.7 us
    pallas_call x1, Pallas kernels, local(): pl.pallas_call(finish_kernel, out_shape=[jax.ShapeDtypeStruct((total, spa...  1.85 us

profile of v5, /device:TPU:1, one launch (start us, length us, event | category | flops | bytes accessed | tf_op | source)
XLA Modules:
  0.0 87.2 jit_solution(11492372901434885257)
XLA Ops:
  0.6 84.7 %shortwave_advection.1 = (f32[576,128]{1,0:T(8,128)}, f32[576,128]{1,0:T(8,128)}) custom-call(f32[2880,128]{1,0:T(8,128)} %bitcast.6, f32[576,128]{1,0:T(8,128)} %bitcast.8, f32[1152,128]{1,0:T(8,128)} %bitcast.7, f32[8,128]{1,0:T(8,128)} %mu_ref.1, f32[8,128]{1,0:T(8,128)} %ground_ref.1, s32[8,128]{1,0:T(8,128)} %day_ref.1, f32[3,72,112]{2,1,0:T(8,128)} %bitcast.9, ...), custom_call_target="tpu_custom_call" | custom-call | tf_op jit(solution)/shard_map/shortwave_advection/pallas_call | solution.py:549
  85.3 1.9 %results.1 = (f32[576,128]{1,0:T(8,128)}, f32[576,128]{1,0:T(8,128)}) custom-call(f32[576,128]{1,0:T(8,128)} %get-tuple-element.6.heat_ref, f32[576,128]{1,0:T(8,128)} %get-tuple-element.7.adv_ref), custom_call_target="tpu_custom_call" | custom-call | tf_op jit(solution)/shard_map/results/pallas_call | solution.py:603
